TPU v7x, 32 devices: a whole 2x2x4 slice. The times are simulated.
32 devices in a mesh: section: 2 (over core), expert: 4 (over z), tensor: 4 (over y, x).
Axes of the slice: x: 2, y: 2, z: 4, core: 2. Of those that a mesh axis runs over, the one named last changes fastest.
Arguments:
- tokens: bfloat16 [32, 197, 768], P('expert'), may hold values from -6 to 6
- batch_order: int32 [4, 8], P('expert'), may hold values from 0 to 7, each once within a row
- gain_attn: float32 [2, 768], P('section'), may hold values from 0.5 to 1.5
- shift_attn: float32 [2, 768], P('section'), may hold values from -3 to 3
- w_qkv: bfloat16 [2, 3, 768, 768], P('section', None, None, 'tensor'), may hold values from -0.21650635 to 0.21650635
- w_out: bfloat16 [2, 768, 768], P('section', 'tensor'), may hold values from -0.875 to 0.875
- gain_moe: float32 [2, 768], P('section'), may hold values from 0.5 to 1.5
- shift_moe: float32 [2, 768], P('section'), may hold values from -3 to 3
- w_router: float32 [2, 768, 8], P('section'), may hold values from -0.04330127 to 0.04330127
- w_in: bfloat16 [2, 8, 768, 3072], P('section', 'expert', None, 'tensor'), may hold values from -0.21875 to 0.21875
- w_back: bfloat16 [2, 8, 3072, 768], P('section', 'expert', 'tensor'), may hold values from -0.4375 to 0.4375
- routes: int32 [2, 32, 197, 2], P('section', 'expert'), may hold values from 0 to 7, as said below
- slots: int32 [2, 32, 197, 2], P('section', 'expert'), may hold values from -1 to 127, as said below
- cotangent: bfloat16 [32, 197, 768], P('expert'), may hold values from -6 to 6
Outputs:
- acts: bfloat16 [2, 32, 197, 768], P('section', 'expert')
- in_grads: float32 [2, 32, 197, 768], P('section', 'expert')
- grad_gain_attn: float32 [2, 768], P('section')
- grad_shift_attn: float32 [2, 768], P('section')
- grad_qkv: float32 [2, 3, 768, 768], P('section', None, None, 'tensor')
- grad_out: float32 [2, 768, 768], P('section', 'tensor')
- grad_gain_moe: float32 [2, 768], P('section')
- grad_shift_moe: float32 [2, 768], P('section')
- grad_router: float32 [2, 768, 8], P('section')
- grad_in: float32 [2, 8, 768, 3072], P('section', 'expert', None, 'tensor')
- grad_back: float32 [2, 8, 3072, 768], P('section', 'expert', 'tensor')
Inputs may be any that keep to these rules, and one draw needn't show every extreme that they name: `routes`: the two experts of a token differ. `slots`: within one layer and one block, choices are ranked first choices by row, then second choices by row, per expert; a choice's slot is its rank, -1 from rank 128 on.
All inputs are finite; a program needn't handle non-finite values.
Results may differ from a plain program's by a relative error of at most 0.019.
Values may be sent and summed in bfloat16 or wider, within the bound.
No kernel may reach another device: no remote copies, remote signals or barrier semaphores. Data moves between devices by JAX's collectives and lax.ppermute only.
A program may use at most 256 MiB of HBM per device.

v0:
```python
import jax
import jax.numpy as jnp
from jax import lax
from jax.sharding import PartitionSpec as P

HEAD = 64
TOPK = 2
SEQ = 197
MB = 4
IMG_MB = 2


NORM_EPS = 1e-06
HIGHEST = lax.Precision.HIGHEST


def from_behind(value, axis, steps):
    count = lax.axis_size(axis)
    first, last = (max(0, -steps), min(count, count - steps))
    return lax.ppermute(value, axis, [(source, source + steps) for source in range(first, last)])


def layer_norm(values, gain, shift):
    centred = values - jnp.mean(values, axis=-1, keepdims=True)
    inverse = lax.rsqrt(jnp.mean(centred * centred, axis=-1, keepdims=True) + NORM_EPS)
    unit_rows = centred * inverse
    return (unit_rows * gain + shift, unit_rows, inverse)


def norm_back(grad, unit_rows, inverse, gain):
    scaled = grad * gain
    inner = (
        scaled
        - jnp.mean(scaled, axis=-1, keepdims=True)
        - unit_rows * jnp.mean(scaled * unit_rows, axis=-1, keepdims=True)
    )
    return (inner * inverse, jnp.sum(grad * unit_rows, axis=0), jnp.sum(grad, axis=0))


def gelu_pair(pre_act):
    normal_cdf = 0.5 * (1.0 + jax.scipy.special.erf(pre_act * 0.7071067811865476))
    density = jnp.exp(-0.5 * pre_act * pre_act) * 0.3989422804014327
    return (pre_act * normal_cdf, normal_cdf + pre_act * density)


def slot_tables(route_block, slot_block, exp_dev, owners, capacity):
    owner_of = route_block // exp_dev
    local_of = route_block % exp_dev
    target = jnp.where(
        slot_block >= 0, local_of * (owners * capacity) + owner_of * capacity + slot_block, -1
    )
    columns = jnp.arange(exp_dev * owners * capacity, dtype=jnp.int32)
    return target[:, :, None] == columns[None, None, :]


def attention_forward(normed_low, wqkv, heads_local, block_rows):
    projected = jnp.einsum(
        "rd,idc->irc", normed_low, wqkv, preferred_element_type=jnp.float32
    ).astype(jnp.bfloat16)
    shaped = projected.reshape(3, IMG_MB, SEQ, heads_local, HEAD)
    scores = jnp.einsum(
        "ishd,ithd->ihst", shaped[0], shaped[1], preferred_element_type=jnp.float32
    ) * HEAD ** (-0.5)
    largest = jnp.max(scores, axis=-1, keepdims=True)
    shifted = jnp.exp(scores - largest)
    row_total = jnp.sum(shifted, axis=-1, keepdims=True)
    attn_probs = (shifted / row_total).astype(jnp.bfloat16)
    mixed_heads = jnp.einsum(
        "ihst,ithd->ishd", attn_probs, shaped[2], preferred_element_type=jnp.float32
    )
    return (
        projected,
        largest + jnp.log(row_total),
        mixed_heads.reshape(block_rows, -1).astype(jnp.bfloat16),
    )


def forward_layer(inputs, weights, route_block, slot_block, layout):
    gain_one, shift_one, wqkv, wout, gain_two, shift_two, wrouter, win, wback = weights
    exp_dev, owners, capacity, heads_local, model_width, block_rows = layout
    normed_a, unit_a, inverse_a = layer_norm(inputs, gain_one, shift_one)
    normed_low = normed_a.astype(jnp.bfloat16)
    projected, logsum, mixed_heads = attention_forward(normed_low, wqkv, heads_local, block_rows)
    attended = lax.psum(jnp.dot(mixed_heads, wout, preferred_element_type=jnp.float32), "tensor")
    hidden = inputs + attended
    normed_m, unit_m, inverse_m = layer_norm(hidden, gain_two, shift_two)
    router_probs = jax.nn.softmax(jnp.dot(normed_m, wrouter, precision=HIGHEST), axis=-1)
    choose = (
        route_block[:, :, None] == jnp.arange(wrouter.shape[1], dtype=jnp.int32)[None, None, :]
    ).astype(jnp.float32)
    gate_values = jnp.sum(router_probs[:, None, :] * choose, axis=-1)
    tables = slot_tables(route_block, slot_block, exp_dev, owners, capacity).astype(jnp.bfloat16)
    sent_rows = jnp.einsum(
        "rks,rd->sd", tables, normed_m.astype(jnp.bfloat16), preferred_element_type=jnp.float32
    ).astype(jnp.bfloat16)
    sent_rows = sent_rows.reshape(exp_dev, owners * capacity, model_width)
    arrived = lax.all_to_all(sent_rows, "expert", split_axis=1, concat_axis=1, tiled=True)
    pre_act = jnp.einsum("erd,edf->erf", arrived, win, preferred_element_type=jnp.float32)
    activated = gelu_pair(pre_act)[0].astype(jnp.bfloat16)
    partial_value = jnp.einsum("erf,efd->erd", activated, wback, preferred_element_type=jnp.float32)
    shares = lax.psum_scatter(partial_value, "tensor", scatter_dimension=2, tiled=True).astype(
        jnp.bfloat16
    )
    quarter = shares.shape[2]
    returned = lax.all_to_all(shares, "expert", split_axis=1, concat_axis=1, tiled=True).reshape(
        -1, quarter
    )
    selected_part = jnp.einsum("rks,sd->rkd", tables, returned, preferred_element_type=jnp.float32)
    hidden_part = lax.dynamic_slice_in_dim(hidden, lax.axis_index("tensor") * quarter, quarter, 1)
    output_part = hidden_part + jnp.sum(gate_values[:, :, None] * selected_part, axis=1)
    output, selected = (
        lax.all_gather(output_part, "tensor", axis=1, tiled=True),
        lax.all_gather(selected_part, "tensor", axis=2, tiled=True),
    )
    saved = (
        unit_a,
        inverse_a,
        normed_low,
        projected,
        logsum,
        mixed_heads,
        unit_m,
        inverse_m,
        normed_m,
        router_probs,
        choose,
        gate_values,
        tables,
        arrived,
        pre_act,
        selected,
    )
    return (output, saved)


def backward_layer(grad_output, weights, saved, layout):
    gain_one, shift_one, wqkv, wout, gain_two, shift_two, wrouter, win, wback = weights
    exp_dev, owners, capacity, heads_local, model_width, block_rows = layout
    (
        unit_a,
        inverse_a,
        normed_low,
        projected,
        logsum,
        mixed_heads,
        unit_m,
        inverse_m,
        normed_m,
        router_probs,
        choose,
        gate_values,
        tables,
        arrived,
        pre_act,
        selected,
    ) = saved
    grad_gates = jnp.sum(grad_output[:, None, :] * selected, axis=-1)
    activated, slope = gelu_pair(pre_act)
    quarter = model_width // lax.axis_size("tensor")
    grad_part = lax.dynamic_slice_in_dim(
        grad_output, lax.axis_index("tensor") * quarter, quarter, 1
    )
    weighted = (gate_values[:, :, None] * grad_part[:, None, :]).astype(jnp.bfloat16)
    grad_sent = jnp.einsum(
        "rks,rkd->sd", tables, weighted, preferred_element_type=jnp.float32
    ).astype(jnp.bfloat16)
    arrived_part = lax.all_to_all(
        grad_sent.reshape(exp_dev, owners * capacity, quarter),
        "expert",
        split_axis=1,
        concat_axis=1,
        tiled=True,
    )
    grad_arrived = lax.all_gather(arrived_part, "tensor", axis=2, tiled=True)
    grad_wback = jnp.einsum(
        "erf,erd->efd",
        activated.astype(jnp.bfloat16),
        grad_arrived,
        preferred_element_type=jnp.float32,
    )
    grad_pre = (
        jnp.einsum("erd,efd->erf", grad_arrived, wback, preferred_element_type=jnp.float32) * slope
    ).astype(jnp.bfloat16)
    grad_win = jnp.einsum("erd,erf->edf", arrived, grad_pre, preferred_element_type=jnp.float32)
    row_terms = jnp.einsum("erf,edf->erd", grad_pre, win, preferred_element_type=jnp.float32)
    grad_share = lax.psum_scatter(row_terms, "tensor", scatter_dimension=2, tiled=True).astype(
        jnp.bfloat16
    )
    home_part = lax.all_to_all(grad_share, "expert", split_axis=1, concat_axis=1, tiled=True)
    grad_home = lax.all_gather(home_part, "tensor", axis=2, tiled=True).reshape(-1, model_width)
    grad_norm_m = jnp.einsum("rks,sd->rd", tables, grad_home, preferred_element_type=jnp.float32)
    grad_probs = jnp.sum(choose * grad_gates[:, :, None], axis=1)
    grad_logits = router_probs * (
        grad_probs - jnp.sum(router_probs * grad_probs, axis=-1, keepdims=True)
    )
    grad_wrouter = jnp.einsum("rd,re->de", normed_m, grad_logits, precision=HIGHEST)
    grad_norm_m = grad_norm_m + jnp.einsum("re,de->rd", grad_logits, wrouter, precision=HIGHEST)
    grad_hidden_ln, grad_gain_two, grad_shift_two = norm_back(
        grad_norm_m, unit_m, inverse_m, gain_two
    )
    grad_hidden = grad_output + grad_hidden_ln
    grad_attn_low = grad_hidden.astype(jnp.bfloat16)
    grad_wout = jnp.einsum(
        "rc,rd->cd", mixed_heads, grad_attn_low, preferred_element_type=jnp.float32
    )
    grad_mixed = jnp.einsum(
        "rd,cd->rc", grad_attn_low, wout, preferred_element_type=jnp.float32
    ).astype(jnp.bfloat16)
    shaped = projected.reshape(3, IMG_MB, SEQ, heads_local, HEAD)
    score_scale = HEAD ** (-0.5)
    scores = (
        jnp.einsum("ishd,ithd->ihst", shaped[0], shaped[1], preferred_element_type=jnp.float32)
        * score_scale
    )
    attn_probs = jnp.exp(scores - logsum)
    grad_heads = grad_mixed.reshape(IMG_MB, SEQ, heads_local, HEAD)
    grad_values = jnp.einsum(
        "ihst,ishd->ithd",
        attn_probs.astype(jnp.bfloat16),
        grad_heads,
        preferred_element_type=jnp.float32,
    )
    grad_weights_soft = jnp.einsum(
        "ishd,ithd->ihst", grad_heads, shaped[2], preferred_element_type=jnp.float32
    )
    grad_scores = (
        attn_probs
        * (grad_weights_soft - jnp.sum(attn_probs * grad_weights_soft, axis=-1, keepdims=True))
    ).astype(jnp.bfloat16)
    grad_queries = (
        jnp.einsum("ihst,ithd->ishd", grad_scores, shaped[1], preferred_element_type=jnp.float32)
        * score_scale
    )
    grad_keys = (
        jnp.einsum("ihst,ishd->ithd", grad_scores, shaped[0], preferred_element_type=jnp.float32)
        * score_scale
    )
    grad_projected = (
        jnp.stack([grad_queries, grad_keys, grad_values])
        .reshape(3, block_rows, -1)
        .astype(jnp.bfloat16)
    )
    grad_wqkv = jnp.einsum(
        "rd,irc->idc", normed_low, grad_projected, preferred_element_type=jnp.float32
    )
    grad_normed_a = lax.psum(
        jnp.einsum("irc,idc->rd", grad_projected, wqkv, preferred_element_type=jnp.float32),
        "tensor",
    )
    grad_input_ln, grad_gain_one, grad_shift_one = norm_back(
        grad_normed_a, unit_a, inverse_a, gain_one
    )
    grad_input = grad_hidden + grad_input_ln
    return (
        grad_input,
        (
            grad_gain_one,
            grad_shift_one,
            grad_wqkv,
            grad_wout,
            grad_gain_two,
            grad_shift_two,
            grad_wrouter,
            grad_win,
            grad_wback,
        ),
    )


def shards(
    tokens,
    batch_order,
    gain_attn,
    shift_attn,
    w_qkv,
    w_out,
    gain_moe,
    shift_moe,
    w_router,
    w_in,
    w_back,
    routes,
    slots,
    cotangent,
):
    section_index = lax.axis_index("section")
    section_count = lax.axis_size("section")
    owners = lax.axis_size("expert")
    exp_dev = w_in.shape[1]
    experts = exp_dev * owners
    model_width = tokens.shape[2]
    block_rows = IMG_MB * SEQ
    capacity = (TOPK * block_rows * 5 // (4 * experts) + 7) // 8 * 8
    heads_local = w_qkv.shape[3] // HEAD
    layout = (exp_dev, owners, capacity, heads_local, model_width, block_rows)
    tick_count = MB + section_count - 1
    image_order = batch_order[0]
    weights = (
        gain_attn[0],
        shift_attn[0],
        w_qkv[0],
        w_out[0],
        gain_moe[0],
        shift_moe[0],
        w_router[0],
        w_in[0],
        w_back[0],
    )
    route_blocks = routes[0].reshape(MB, block_rows, TOPK)
    slot_blocks = slots[0].reshape(MB, block_rows, TOPK)
    inbound = jnp.zeros((block_rows, model_width), jnp.bfloat16)
    acts_store = jnp.zeros((MB, block_rows, model_width), jnp.bfloat16)
    kept_ticks = []
    for tick_index in range(tick_count):
        micro_index = tick_index - section_index
        active = (micro_index >= 0) & (micro_index < MB)
        clipped = jnp.clip(micro_index, 0, MB - 1)
        if tick_index < MB:
            fresh = jnp.take(
                tokens, image_order[tick_index * IMG_MB : (tick_index + 1) * IMG_MB], axis=0
            ).reshape(block_rows, model_width)
        else:
            fresh = jnp.zeros((block_rows, model_width), jnp.bfloat16)
        inputs = jnp.where(section_index == 0, fresh, inbound).astype(jnp.float32)
        route_block = lax.dynamic_index_in_dim(route_blocks, clipped, 0, keepdims=False)
        slot_block = lax.dynamic_index_in_dim(slot_blocks, clipped, 0, keepdims=False)
        output, saved = forward_layer(inputs, weights, route_block, slot_block, layout)
        output_low = output.astype(jnp.bfloat16)
        previous = lax.dynamic_index_in_dim(acts_store, clipped, 0, keepdims=False)
        acts_store = lax.dynamic_update_index_in_dim(
            acts_store, jnp.where(active, output_low, previous), clipped, 0
        )
        kept_ticks.append((saved, active, clipped))
        if tick_index + 1 < tick_count:
            inbound = from_behind(output_low, "section", 1)
    targets = jnp.take(cotangent, image_order, axis=0).reshape(MB, block_rows, model_width)
    grad_inbound = jnp.zeros((block_rows, model_width), jnp.bfloat16)
    grad_store = jnp.zeros((MB, block_rows, model_width), jnp.float32)
    totals = tuple((jnp.zeros(weight_item.shape, jnp.float32) for weight_item in weights))
    for back_index in range(tick_count):
        saved, active, clipped = kept_ticks[tick_count - 1 - back_index]
        target_rows = lax.dynamic_index_in_dim(targets, clipped, 0, keepdims=False)
        grad_output = jnp.where(
            section_index == section_count - 1, target_rows, grad_inbound
        ).astype(jnp.float32)
        grad_input, layer_grads = backward_layer(grad_output, weights, saved, layout)
        totals = tuple(
            (
                running + jnp.where(active, fresh_grad, 0.0)
                for running, fresh_grad in zip(totals, layer_grads)
            )
        )
        previous = lax.dynamic_index_in_dim(grad_store, clipped, 0, keepdims=False)
        grad_store = lax.dynamic_update_index_in_dim(
            grad_store, jnp.where(active, grad_input, previous), clipped, 0
        )
        if back_index + 1 < tick_count:
            grad_inbound = from_behind(grad_input.astype(jnp.bfloat16), "section", -1)
    shared = lax.psum(
        (totals[0], totals[1], totals[2], totals[3], totals[4], totals[5], totals[6]), "expert"
    )
    image_count = MB * IMG_MB
    acts_image = (
        jnp.zeros((image_count, SEQ, model_width), jnp.bfloat16)
        .at[image_order]
        .set(acts_store.reshape(image_count, SEQ, model_width))
    )
    grads_image = (
        jnp.zeros((image_count, SEQ, model_width), jnp.float32)
        .at[image_order]
        .set(grad_store.reshape(image_count, SEQ, model_width))
    )
    return (
        acts_image[None],
        grads_image[None],
        shared[0][None],
        shared[1][None],
        shared[2][None],
        shared[3][None],
        shared[4][None],
        shared[5][None],
        shared[6][None],
        totals[7][None],
        totals[8][None],
    )


def solution(mesh):
    return jax.shard_map(
        shards,
        mesh=mesh,
        in_specs=(
            P("expert", None, None),
            P("expert", None),
            P("section", None),
            P("section", None),
            P("section", None, None, "tensor"),
            P("section", "tensor", None),
            P("section", None),
            P("section", None),
            P("section", None, None),
            P("section", "expert", None, "tensor"),
            P("section", "expert", "tensor", None),
            P("section", "expert", None, None),
            P("section", "expert", None, None),
            P("expert", None, None),
        ),
        out_specs=(
            P("section", "expert", None, None),
            P("section", "expert", None, None),
            P("section", None),
            P("section", None),
            P("section", None, None, "tensor"),
            P("section", "tensor", None),
            P("section", None),
            P("section", None),
            P("section", None, None),
            P("section", "expert", None, "tensor"),
            P("section", "expert", "tensor", None),
        ),
        check_vma=False,
    )
```

profile of v0, /device:TPU:0, one launch (start us, length us, event | category | flops | bytes accessed | tf_op | source)
XLA Modules:
  0.0 2706.1 jit_solution(5228686551862741128)
XLA Ops:
  36.3 55.6 %all-reduce.14.cloned.1.call-done = f32[394,768]{0,1:T(8,128)} async-done(((f32[394,768]{0,1:T(8,128)}), f32[394,768]{0,1:T(8,128)}) %all-reduce.14.cloned.1.call-update) | async-done | bytes 1210384 | tf_op jit(solution)/shard_map/psum | solution.py:84
  98.9 41.3 %all_to_all.100 = bf16[2,512,768]{2,0,1:T(2,128)(2,1)} all-to-all(bf16[2,512,768]{2,0,1:T(2,128)(2,1)S(1)} %copy.1194), channel_id=1, replica_groups=mesh['section'=2,'expert'=4,'tensor'=4] {'expert'}, dimensions={1} | all-to-all | bytes 3145728 | tf_op jit(solution)/shard_map/all_to_all | solution.py:97
  153.5 42.1 %reduce-scatter.11.cloned.1.call-done = f32[2,512,192]{1,2,0:T(8,128)} async-done(((f32[2,512,768]{1,2,0:T(8,128)}), f32[2,512,192]{1,2,0:T(8,128)}) %reduce-scatter.11.cloned.1.call-update) | async-done | bytes 786448 | tf_op jit(solution)/shard_map/reduce_scatter | solution.py:101
  272.3 57.2 %all-reduce.16.cloned.1.call-done = f32[394,768]{0,1:T(8,128)} async-done(((f32[394,768]{0,1:T(8,128)}), f32[394,768]{0,1:T(8,128)}) %all-reduce.16.cloned.1.call-update) | async-done | bytes 1210384 | tf_op jit(solution)/shard_map/psum | solution.py:84
  336.0 41.3 %all_to_all.101 = bf16[2,512,768]{2,0,1:T(2,128)(2,1)} all-to-all(bf16[2,512,768]{2,0,1:T(2,128)(2,1)S(1)} %copy.1211), channel_id=1, replica_groups=mesh['section'=2,'expert'=4,'tensor'=4] {'expert'}, dimensions={1} | all-to-all | bytes 3145728 | tf_op jit(solution)/shard_map/all_to_all | solution.py:97
  392.2 42.2 %reduce-scatter.13.cloned.1.call-done = f32[2,512,192]{1,2,0:T(8,128)} async-done(((f32[2,512,768]{1,2,0:T(8,128)}), f32[2,512,192]{1,2,0:T(8,128)}) %reduce-scatter.13.cloned.1.call-update) | async-done | bytes 786448 | tf_op jit(solution)/shard_map/reduce_scatter | solution.py:101
  503.5 58.1 %all-reduce.18.cloned.1.call-done = f32[394,768]{0,1:T(8,128)} async-done(((f32[394,768]{0,1:T(8,128)}), f32[394,768]{0,1:T(8,128)}) %all-reduce.18.cloned.1.call-update) | async-done | bytes 1210384 | tf_op jit(solution)/shard_map/psum | solution.py:84
  568.0 41.3 %all_to_all.102 = bf16[2,512,768]{2,0,1:T(2,128)(2,1)} all-to-all(bf16[2,512,768]{2,0,1:T(2,128)(2,1)S(1)} %copy.1229), channel_id=1, replica_groups=mesh['section'=2,'expert'=4,'tensor'=4] {'expert'}, dimensions={1} | all-to-all | bytes 3145728 | tf_op jit(solution)/shard_map/all_to_all | solution.py:97
  624.3 42.2 %reduce-scatter.15.cloned.1.call-done = f32[2,512,192]{1,2,0:T(8,128)} async-done(((f32[2,512,768]{1,2,0:T(8,128)}), f32[2,512,192]{1,2,0:T(8,128)}) %reduce-scatter.15.cloned.1.call-update) | async-done | bytes 786448 | tf_op jit(solution)/shard_map/reduce_scatter | solution.py:101
  715.2 58.7 %all-reduce.20.cloned.1.call-done = f32[394,768]{0,1:T(8,128)} async-done(((f32[394,768]{0,1:T(8,128)}), f32[394,768]{0,1:T(8,128)}) %all-reduce.20.cloned.1.call-update) | async-done | bytes 1210384 | tf_op jit(solution)/shard_map/psum | solution.py:84
  780.3 41.5 %all_to_all.103 = bf16[2,512,768]{2,0,1:T(2,128)(2,1)} all-to-all(bf16[2,512,768]{2,0,1:T(2,128)(2,1)S(1)} %copy.1247), channel_id=1, replica_groups=mesh['section'=2,'expert'=4,'tensor'=4] {'expert'}, dimensions={1} | all-to-all | bytes 3145728 | tf_op jit(solution)/shard_map/all_to_all | solution.py:97
  836.7 42.2 %reduce-scatter.17.cloned.1.call-done = f32[2,512,192]{1,2,0:T(8,128)} async-done(((f32[2,512,768]{1,2,0:T(8,128)}), f32[2,512,192]{1,2,0:T(8,128)}) %reduce-scatter.17.cloned.1.call-update) | async-done | bytes 786448 | tf_op jit(solution)/shard_map/reduce_scatter | solution.py:101
  925.6 58.5 %all-reduce.22.cloned.1.call-done = f32[394,768]{0,1:T(8,128)} async-done(((f32[394,768]{0,1:T(8,128)}), f32[394,768]{0,1:T(8,128)}) %all-reduce.22.cloned.1.call-update) | async-done | bytes 1210384 | tf_op jit(solution)/shard_map/psum | solution.py:84
  989.2 41.3 %all_to_all.104 = bf16[2,512,768]{2,0,1:T(2,128)(2,1)} all-to-all(bf16[2,512,768]{2,0,1:T(2,128)(2,1)S(1)} %copy.1263), channel_id=1, replica_groups=mesh['section'=2,'expert'=4,'tensor'=4] {'expert'}, dimensions={1} | all-to-all | bytes 3145728 | tf_op jit(solution)/shard_map/all_to_all | solution.py:97
  1043.9 42.1 %reduce-scatter.19.cloned.1.call-done = f32[2,512,192]{1,2,0:T(8,128)} async-done(((f32[2,512,768]{1,2,0:T(8,128)}), f32[2,512,192]{1,2,0:T(8,128)}) %reduce-scatter.19.cloned.1.call-update) | async-done | bytes 786448 | tf_op jit(solution)/shard_map/reduce_scatter | solution.py:101
  1181.5 29.2 %all-gather.16.cloned.1.call-done = bf16[2,512,768]{1,2,0:T(8,128)(2,1)} async-done(((bf16[2,512,192]{1,2,0:T(8,128)(2,1)}), bf16[2,512,768]{1,2,0:T(8,128)(2,1)}) %all-gather.16.cloned.1.call-update) | async-done | bytes 1572880 | tf_op jit(solution)/shard_map/all_gather | solution.py:174
  1220.5 44.0 %reduce-scatter.21.cloned.1.call-done = f32[2,512,192]{1,2,0:T(8,128)} async-done(((f32[2,512,768]{1,2,0:T(8,128)}), f32[2,512,192]{1,2,0:T(8,128)}) %reduce-scatter.21.cloned.1.call-update) | async-done | bytes 786448 | tf_op jit(solution)/shard_map/reduce_scatter | solution.py:186
  1338.4 60.8 %all-reduce.24.cloned.1.call-done = f32[394,768]{0,1:T(8,128)} async-done(((f32[394,768]{0,1:T(8,128)}), f32[394,768]{0,1:T(8,128)}) %all-reduce.24.cloned.1.call-update) | async-done | bytes 1210384 | tf_op jit(solution)/shard_map/psum | solution.py:246
  1436.8 28.9 %all-gather.22.cloned.1.call-done = bf16[2,512,768]{1,2,0:T(8,128)(2,1)} async-done(((bf16[2,512,192]{1,2,0:T(8,128)(2,1)}), bf16[2,512,768]{1,2,0:T(8,128)(2,1)}) %all-gather.22.cloned.1.call-update) | async-done | bytes 1572880 | tf_op jit(solution)/shard_map/all_gather | solution.py:174
  1476.1 43.4 %reduce-scatter.23.cloned.1.call-done = f32[2,512,192]{1,2,0:T(8,128)} async-done(((f32[2,512,768]{1,2,0:T(8,128)}), f32[2,512,192]{1,2,0:T(8,128)}) %reduce-scatter.23.cloned.1.call-update) | async-done | bytes 786448 | tf_op jit(solution)/shard_map/reduce_scatter | solution.py:186
  1571.2 27.2 %all-gather.24.cloned.1.call-done = bf16[2,512,768]{1,0,2:T(2,128)(2,1)} async-done(((bf16[2,512,192]{1,0,2:T(2,128)(2,1)}), bf16[2,512,768]{1,0,2:T(2,128)(2,1)}) %all-gather.24.cloned.1.call-update) | async-done | bytes 1572880 | tf_op jit(solution)/shard_map/all_gather | solution.py:190
  1624.9 52.6 %all-reduce.26.cloned.1.call-done = f32[394,768]{0,1:T(8,128)} async-done(((f32[394,768]{0,1:T(8,128)}), f32[394,768]{0,1:T(8,128)}) %all-reduce.26.cloned.1.call-update) | async-done | bytes 1210384 | tf_op jit(solution)/shard_map/psum | solution.py:246
  1716.8 29.1 %all-gather.28.cloned.1.call-done = bf16[2,512,768]{1,2,0:T(8,128)(2,1)} async-done(((bf16[2,512,192]{1,2,0:T(8,128)(2,1)}), bf16[2,512,768]{1,2,0:T(8,128)(2,1)}) %all-gather.28.cloned.1.call-update) | async-done | bytes 1572880 | tf_op jit(solution)/shard_map/all_gather | solution.py:174
  1756.4 43.3 %reduce-scatter.25.cloned.1.call-done = f32[2,512,192]{1,2,0:T(8,128)} async-done(((f32[2,512,768]{1,2,0:T(8,128)}), f32[2,512,192]{1,2,0:T(8,128)}) %reduce-scatter.25.cloned.1.call-update) | async-done | bytes 786448 | tf_op jit(solution)/shard_map/reduce_scatter | solution.py:186
  1905.2 52.5 %all-reduce.28.cloned.1.call-done = f32[394,768]{0,1:T(8,128)} async-done(((f32[394,768]{0,1:T(8,128)}), f32[394,768]{0,1:T(8,128)}) %all-reduce.28.cloned.1.call-update) | async-done | bytes 1210384 | tf_op jit(solution)/shard_map/psum | solution.py:246
  1997.1 28.9 %all-gather.34.cloned.1.call-done = bf16[2,512,768]{1,2,0:T(8,128)(2,1)} async-done(((bf16[2,512,192]{1,2,0:T(8,128)(2,1)}), bf16[2,512,768]{1,2,0:T(8,128)(2,1)}) %all-gather.34.cloned.1.call-update) | async-done | bytes 1572880 | tf_op jit(solution)/shard_map/all_gather | solution.py:174
  2036.5 43.3 %reduce-scatter.27.cloned.1.call-done = f32[2,512,192]{1,2,0:T(8,128)} async-done(((f32[2,512,768]{1,2,0:T(8,128)}), f32[2,512,192]{1,2,0:T(8,128)}) %reduce-scatter.27.cloned.1.call-update) | async-done | bytes 786448 | tf_op jit(solution)/shard_map/reduce_scatter | solution.py:186
  2131.6 27.2 %all-gather.36.cloned.1.call-done = bf16[2,512,768]{1,0,2:T(2,128)(2,1)} async-done(((bf16[2,512,192]{1,0,2:T(2,128)(2,1)}), bf16[2,512,768]{1,0,2:T(2,128)(2,1)}) %all-gather.36.cloned.1.call-update) | async-done | bytes 1572880 | tf_op jit(solution)/shard_map/all_gather | solution.py:190
  2198.3 49.9 %all-reduce.30.cloned.1.call-done = f32[394,768]{0,1:T(8,128)} async-done(((f32[394,768]{0,1:T(8,128)}), f32[394,768]{0,1:T(8,128)}) %all-reduce.30.cloned.1.call-update) | async-done | bytes 1210384 | tf_op jit(solution)/shard_map/psum | solution.py:246
  2294.8 29.1 %all-gather.40.cloned.1.call-done = bf16[2,512,768]{1,2,0:T(8,128)(2,1)} async-done(((bf16[2,512,192]{1,2,0:T(8,128)(2,1)}), bf16[2,512,768]{1,2,0:T(8,128)(2,1)}) %all-gather.40.cloned.1.call-update) | async-done | bytes 1572880 | tf_op jit(solution)/shard_map/all_gather | solution.py:174
  2554.9 41.4 %all-reduce.32.cloned.1.call-done = f32[394,768]{0,1:T(8,128)} async-done(((f32[394,768]{0,1:T(8,128)}), f32[394,768]{0,1:T(8,128)}) %all-reduce.32.cloned.1.call-update) | async-done | bytes 1210384 | tf_op jit(solution)/shard_map/psum | solution.py:246
  2649.5 45.9 %all-reduce.34.cloned.1.call-done = (f32[1,3,768,192]{2,3,1,0:T(8,128)}, f32[1,192,768]{2,1,0:T(8,128)}) async-done(((f32[1,3,768,192]{2,3,1,0:T(8,128)}, f32[1,192,768]{2,1,0:T(8,128)}), (f32[1,3,768,192]{2,3,1,0:T(8,128)}, f32[1,192,768]{2,1,0:T(8,128)})) %all-reduce.34.cloned.1.call-update) | async-done | bytes 2359312 | tf_op jit(solution)/shard_map/psum | solution.py:359
  (1434 shorter events, 1304.0 us)
Async XLA Ops:
  7.2 84.7 %all-reduce.14.cloned.1.call-start = ((), (), s32[]{:S(2)}) async-start(), calls=%async_computation.30 | async-start | bytes 3145728 | tf_op jit(solution)/shard_map/psum | solution.py:84
  28.2 167.4 %reduce-scatter.11.cloned.1.call-start = ((), (), s32[]{:S(2)}) async-start(), calls=%async_computation.31 | async-start | bytes 3932160 | tf_op jit(solution)/shard_map/reduce_scatter | solution.py:101
  202.5 127.0 %all-reduce.16.cloned.1.call-start = ((), (), s32[]{:S(2)}) async-start(), calls=%async_computation.32 | async-start | bytes 3145728 | tf_op jit(solution)/shard_map/psum | solution.py:84
  270.1 164.3 %reduce-scatter.13.cloned.1.call-start = ((), (), s32[]{:S(2)}) async-start(), calls=%async_computation.33 | async-start | bytes 3932160 | tf_op jit(solution)/shard_map/reduce_scatter | solution.py:101
  441.2 120.3 %all-reduce.18.cloned.1.call-start = ((), (), s32[]{:S(2)}) async-start(), calls=%async_computation.34 | async-start | bytes 3145728 | tf_op jit(solution)/shard_map/psum | solution.py:84
  502.1 164.3 %reduce-scatter.15.cloned.1.call-start = ((), (), s32[]{:S(2)}) async-start(), calls=%async_computation.35 | async-start | bytes 3932160 | tf_op jit(solution)/shard_map/reduce_scatter | solution.py:101
  673.3 100.6 %all-reduce.20.cloned.1.call-start = ((), (), s32[]{:S(2)}) async-start(), calls=%async_computation.36 | async-start | bytes 3145728 | tf_op jit(solution)/shard_map/psum | solution.py:84
  713.9 165.0 %reduce-scatter.17.cloned.1.call-start = ((), (), s32[]{:S(2)}) async-start(), calls=%async_computation.37 | async-start | bytes 3932160 | tf_op jit(solution)/shard_map/reduce_scatter | solution.py:101
  885.8 98.4 %all-reduce.22.cloned.1.call-start = ((), (), s32[]{:S(2)}) async-start(), calls=%async_computation.38 | async-start | bytes 3145728 | tf_op jit(solution)/shard_map/psum | solution.py:84
  924.7 161.3 %reduce-scatter.19.cloned.1.call-start = ((), (), s32[]{:S(2)}) async-start(), calls=%async_computation.39 | async-start | bytes 3932160 | tf_op jit(solution)/shard_map/reduce_scatter | solution.py:101
  1043.8 109.5 %all-gather.20.cloned.1.call-start = ((), (), s32[]{:S(2)}) async-start(), calls=%async_computation.43 | async-start | bytes 3932160 | tf_op jit(solution)/shard_map/all_gather | solution.py:113
  1111.2 99.5 %all-gather.16.cloned.1.call-start = ((), (), s32[]{:S(2)}) async-start(), calls=%async_computation.40 | async-start | bytes 1966080 | tf_op jit(solution)/shard_map/all_gather | solution.py:174
  1181.4 83.1 %reduce-scatter.21.cloned.1.call-start = ((), (), s32[]{:S(2)}) async-start(), calls=%async_computation.41 | async-start | bytes 3932160 | tf_op jit(solution)/shard_map/reduce_scatter | solution.py:186
  1220.4 98.8 %all-gather.18.cloned.1.call-start = ((), (), s32[]{:S(2)}) async-start(), calls=%async_computation.42 | async-start | bytes 1966080 | tf_op jit(solution)/shard_map/all_gather | solution.py:190
  1290.1 109.1 %all-reduce.24.cloned.1.call-start = ((), (), s32[]{:S(2)}) async-start(), calls=%async_computation.44 | async-start | bytes 3145728 | tf_op jit(solution)/shard_map/psum | solution.py:246
  1338.3 127.4 %all-gather.22.cloned.1.call-start = ((), (), s32[]{:S(2)}) async-start(), calls=%async_computation.45 | async-start | bytes 1966080 | tf_op jit(solution)/shard_map/all_gather | solution.py:174
  1475.5 89.6 %all-gather.26.cloned.1.call-start = ((), (), s32[]{:S(2)}) async-start(), calls=%async_computation.48 | async-start | bytes 3932160 | tf_op jit(solution)/shard_map/all_gather | solution.py:113
  1476.1 122.3 %all-gather.24.cloned.1.call-start = ((), (), s32[]{:S(2)}) async-start(), calls=%async_computation.47 | async-start | bytes 1966080 | tf_op jit(solution)/shard_map/all_gather | solution.py:190
  1545.1 132.5 %all-reduce.26.cloned.1.call-start = ((), (), s32[]{:S(2)}) async-start(), calls=%async_computation.49 | async-start | bytes 3145728 | tf_op jit(solution)/shard_map/psum | solution.py:246
  1616.7 129.2 %all-gather.28.cloned.1.call-start = ((), (), s32[]{:S(2)}) async-start(), calls=%async_computation.50 | async-start | bytes 1966080 | tf_op jit(solution)/shard_map/all_gather | solution.py:174
  1755.7 89.8 %all-gather.32.cloned.1.call-start = ((), (), s32[]{:S(2)}) async-start(), calls=%async_computation.53 | async-start | bytes 3932160 | tf_op jit(solution)/shard_map/all_gather | solution.py:113
  1756.4 122.2 %all-gather.30.cloned.1.call-start = ((), (), s32[]{:S(2)}) async-start(), calls=%async_computation.52 | async-start | bytes 1966080 | tf_op jit(solution)/shard_map/all_gather | solution.py:190
  1825.3 132.4 %all-reduce.28.cloned.1.call-start = ((), (), s32[]{:S(2)}) async-start(), calls=%async_computation.54 | async-start | bytes 3145728 | tf_op jit(solution)/shard_map/psum | solution.py:246
  1896.8 129.2 %all-gather.34.cloned.1.call-start = ((), (), s32[]{:S(2)}) async-start(), calls=%async_computation.55 | async-start | bytes 1966080 | tf_op jit(solution)/shard_map/all_gather | solution.py:174
  2035.7 89.8 %all-gather.38.cloned.1.call-start = ((), (), s32[]{:S(2)}) async-start(), calls=%async_computation.58 | async-start | bytes 3932160 | tf_op jit(solution)/shard_map/all_gather | solution.py:113
  2036.5 122.3 %all-gather.36.cloned.1.call-start = ((), (), s32[]{:S(2)}) async-start(), calls=%async_computation.57 | async-start | bytes 1966080 | tf_op jit(solution)/shard_map/all_gather | solution.py:190
  2105.4 142.8 %all-reduce.30.cloned.1.call-start = ((), (), s32[]{:S(2)}) async-start(), calls=%async_computation.59 | async-start | bytes 3145728 | tf_op jit(solution)/shard_map/psum | solution.py:246
  2187.3 136.5 %all-gather.40.cloned.1.call-start = ((), (), s32[]{:S(2)}) async-start(), calls=%async_computation.60 | async-start | bytes 1966080 | tf_op jit(solution)/shard_map/all_gather | solution.py:174
  2294.7 165.7 %reduce-scatter.29.cloned.1.call-start = ((), (), s32[]{:S(2)}) async-start(), calls=%async_computation.61 | async-start | bytes 3932160 | tf_op jit(solution)/shard_map/reduce_scatter | solution.py:186
  2333.7 148.8 %all-gather.44.cloned.1.call-start = ((), (), s32[]{:S(2)}) async-start(), calls=%async_computation.63 | async-start | bytes 3932160 | tf_op jit(solution)/shard_map/all_gather | solution.py:113
  2482.2 114.1 %all-reduce.32.cloned.1.call-start = ((), (), s32[]{:S(2)}) async-start(), calls=%async_computation.64 | async-start | bytes 3145728 | tf_op jit(solution)/shard_map/psum | solution.py:246
  2535.4 159.9 %all-reduce.34.cloned.1.call-start = ((), (), s32[]{:S(2)}) async-start(), calls=%async_computation.65 | async-start | bytes 4718592 | tf_op jit(solution)/shard_map/psum | solution.py:359
  (398 other events, 6997.4 us)
Sparse Core Ops, SparseCore 0:
  28.3 63.4 all-reduce.13
  153.5 42.0 reduce-scatter.10
  270.2 59.2 all-reduce.15
  392.3 42.0 reduce-scatter.12
  502.2 59.2 all-reduce.17
  624.4 42.0 reduce-scatter.14
  714.0 59.8 all-reduce.19
  836.8 42.0 reduce-scatter.16
  924.8 59.2 all-reduce.21
  1044.0 42.0 reduce-scatter.18
  1111.3 41.9 all-gather.19
  1181.6 29.0 all-gather.15
  1220.6 43.8 reduce-scatter.20
  1338.4 60.7 all-reduce.23
  1475.6 43.8 reduce-scatter.22
  1521.2 43.8 all-gather.25
  1567.5 30.8 all-gather.23
  1616.8 60.7 all-reduce.25
  1716.8 28.9 all-gather.27
  1755.8 43.8 reduce-scatter.24
  1801.6 43.8 all-gather.31
  1847.7 30.8 all-gather.29
  1896.9 60.7 all-reduce.27
  2035.9 43.8 reduce-scatter.26
  2081.6 43.8 all-gather.37
  2127.9 30.8 all-gather.35
  2187.4 60.7 all-reduce.29
  2333.8 43.8 reduce-scatter.28
  2379.4 45.9 all-gather.43
  2482.2 31.2 all-gather.41
  2535.5 60.7 all-reduce.31
  2599.1 96.1 all-reduce.33
  (4 shorter events, 115.6 us)
where the time goes:
time: 2720 us; the launch traced here: 2710 us
  waiting for transfers between devices  1370 us (50%)
  blocking collectives  482 us (18%)
  local copies, waits for them, and re-layouts  397 us (15%)
  matrix products  269 us (10%)
  other arithmetic  125 us (5%)
  starting transfers between devices  39.8 us (1%)
    psum x5, waiting for transfers between devices, forward_layer(): lax.psum(jnp.dot(mixed_heads, wout, preferred_element_type=jnp.float32),...  288 us
    psum x5, waiting for transfers between devices, backward_layer(): lax.psum(jnp.einsum('irc,idc->rd', grad_projected, wqkv, preferred_elemen...  257 us
    reduce_scatter x5, waiting for transfers between devices, forward_layer(): lax.psum_scatter(partial_value, 'tensor', scatter_dimension=2, tiled=True)  211 us
    all_to_all x5, blocking collectives, forward_layer(): lax.all_to_all(sent_rows, 'expert', split_axis=1, concat_axis=1, tiled=True)  207 us
    reduce_scatter x5, waiting for transfers between devices, backward_layer(): lax.psum_scatter(row_terms, 'tensor', scatter_dimension=2, tiled=True)  174 us
    all_gather x5, waiting for transfers between devices, backward_layer(): grad_arrived = lax.all_gather(arrived_part, 'tensor', axis=2, tiled=True)  145 us
    all_gather x5, waiting for transfers between devices, backward_layer(): lax.all_gather(home_part, 'tensor', axis=2, tiled=True)  120 us
    all_to_all x5, blocking collectives, backward_layer(): lax.all_to_all(grad_sent.reshape(exp_dev, owners * capacity, quarter), 'e...  96 us
  transfers between devices with their start and end apart: 49, of which 43 were waited for; matrix products, arithmetic and copies ran while one was open for 12% of the time, Pallas kernels for 0%

commit v1 on v0

v1 whole, which is shorter than its diff:
```python
from types import SimpleNamespace

import jax
import jax.numpy as jnp
from jax import lax
from jax.experimental import pallas as pl
from jax.experimental.pallas import tpu as pltpu
from jax.sharding import PartitionSpec as P


HEAD = 64
TOPK = 2
MB = 4
IMG_MB = 2
NORM_EPS = 1e-06
HIGHEST = lax.Precision.HIGHEST
LOW = jnp.bfloat16
F32 = jnp.float32


SECTION, EXPERT, TENSOR = "section", "expert", "tensor"


def swap(value):
    return lax.ppermute(value, SECTION, [(0, 1), (1, 0)])


def across(value, flip):
    count = lax.axis_size(TENSOR)
    return lax.ppermute(value, TENSOR, [(i, i ^ flip) for i in range(count)])


def along(value, flip):
    count = lax.axis_size(EXPERT)
    return lax.ppermute(value, EXPERT, [(i, i ^ flip) for i in range(count)])


def hop(value, flip_expert, flip_tensor):
    owners, count = lax.axis_size(EXPERT), lax.axis_size(TENSOR)
    pairs = [
        (e * count + t, (e ^ flip_expert) * count + (t ^ flip_tensor))
        for e in range(owners)
        for t in range(count)
    ]
    return lax.ppermute(value, (EXPERT, TENSOR), pairs)


def to_sibling(value, layer):
    return lax.ppermute(value, SECTION, [(layer, 1 - layer)])


def to_owner(value, layer):
    return lax.ppermute(value, SECTION, [(1 - layer, layer)])


def V(value):
    return value, pltpu.VMEM


def A(value):
    return value, pl.ANY


def S(value):
    return value, pltpu.SMEM


def O(shape, dtype, count=None, space=pltpu.VMEM):
    return shape, dtype, count, space


def named(names, flat):
    result, place = {}, 0
    for key, count in names:
        if count is None:
            result[key] = flat[place]
            place += 1
        else:
            result[key] = list(flat[place : place + count])
            place += count
    return result


def run(body, ins, outs, scratch=None, flops=0):
    scratch = scratch or {}
    arrays, in_specs, in_names = [], [], []
    for key, (value, space) in ins.items():
        many = isinstance(value, (list, tuple))
        in_names.append((key, len(value) if many else None))
        for item in value if many else [value]:
            arrays.append(item)
            in_specs.append(pl.BlockSpec(memory_space=space))
    shapes, out_specs, out_names = [], [], []
    for key, (shape, dtype, count, space) in outs.items():
        out_names.append((key, count))
        for _ in range(1 if count is None else count):
            shapes.append(jax.ShapeDtypeStruct(shape, dtype))
            out_specs.append(pl.BlockSpec(memory_space=space))
    n_in, n_out = len(arrays), len(shapes)

    def kernel(*refs):
        names = named(in_names, refs[:n_in])
        names.update(named(out_names, refs[n_in : n_in + n_out]))
        names.update(zip(scratch.keys(), refs[n_in + n_out :]))
        body(SimpleNamespace(**names))

    moved = sum(a.size * a.dtype.itemsize for a in arrays)
    moved += sum(s.size * jnp.dtype(s.dtype).itemsize for s in shapes)
    cost = pl.CostEstimate(flops=int(flops), bytes_accessed=int(moved), transcendentals=0)
    results = pl.pallas_call(
        kernel,
        out_shape=tuple(shapes),
        in_specs=in_specs,
        out_specs=tuple(out_specs),
        scratch_shapes=list(scratch.values()),
        cost_estimate=cost,
    )(*arrays)
    return SimpleNamespace(**named(out_names, results))


def dot(left, right, precision=None):
    return jnp.dot(left, right, preferred_element_type=F32, precision=precision)


def dot_nt(left, right, precision=None):
    return lax.dot_general(
        left, right, (((1,), (1,)), ((), ())), preferred_element_type=F32, precision=precision
    )


def dot_tn(left, right, precision=None):
    return lax.dot_general(
        left, right, (((0,), (0,)), ((), ())), preferred_element_type=F32, precision=precision
    )


def unit_rows(values):
    centred = values - jnp.mean(values, axis=-1, keepdims=True)
    inverse = lax.rsqrt(jnp.mean(centred * centred, axis=-1, keepdims=True) + NORM_EPS)
    return centred * inverse, inverse


def norm_back(grad, unit, inverse, gain):
    scaled = grad * gain
    inner = (
        scaled
        - jnp.mean(scaled, axis=-1, keepdims=True)
        - unit * jnp.mean(scaled * unit, axis=-1, keepdims=True)
    )
    return inner * inverse


def gelu_pair(pre_act):
    normal_cdf = 0.5 * (1.0 + lax.erf(pre_act * 0.7071067811865476))
    density = jnp.exp(-0.5 * pre_act * pre_act) * 0.3989422804014327
    return pre_act * normal_cdf, normal_cdf + pre_act * density


def fetch(owner, direct, forwarded, target, sem):
    @pl.when(owner)
    def _():
        pltpu.make_async_copy(direct, target, sem).start()

    @pl.when(jnp.logical_not(owner))
    def _():
        pltpu.make_async_copy(forwarded, target, sem).start()


def arrived(target, sem):
    pltpu.make_async_copy(target, target, sem).wait()


def image_of(ns, flip, other):
    return ns.order[(ns.info[2] ^ flip) * IMG_MB + (ns.info[0] ^ other)]


def lanes(count):
    return lax.broadcasted_iota(jnp.int32, (1, count), 1)


def one_hot(index, count):
    return index == lanes(count)


def plan(cfg, picks, others):
    size = cfg.padded

    def body(ns):
        first, expert, mine = ns.info[0] == 0, ns.info[1], ns.info[3]
        for layer in range(2):
            here = ns.info[0] == layer
            picks = jnp.where(here, ns.picks[...], ns.others[...])
            pairs = []
            for i in range(2):
                part = picks[4 * i : 4 * i + 4, :]
                pairs.append((part[0:TOPK, :], part[TOPK:, :]))
            own = [jnp.where(first, low, high) for low, high in pairs]
            other = [jnp.where(first, high, low) for low, high in pairs]
            for i, (route, slot) in enumerate((own, other)):
                route = jnp.maximum(route, 0)
                chunk = (((route >> 1) ^ expert) << 1) + ((route & 1) ^ mine)
                half = jnp.where(slot >= cfg.rows, 1, 0)
                index = chunk * cfg.rows + slot - half * cfg.rows
                sent = (slot >= 0) & (half == ns.info[0])
                ns.targets[layer][TOPK * i : TOPK * (i + 1), :] = jnp.where(sent, index, -1)
                if i == 0:
                    full = jnp.where(slot >= 0, (half ^ ns.info[0]) * cfg.slots + index, -1)
                    ns.wide[...] = jnp.zeros_like(ns.wide)
                    ns.wide[0:TOPK, 0:size] = route.astype(F32)
                    ns.wide[TOPK : 2 * TOPK, 0:size] = full.astype(F32)
                    tall = ns.wide[...].T
                    ns.columns[layer][...] = tall[0:size, 0 : 2 * TOPK].astype(jnp.int32)

    ins = dict(info=S(cfg.info), picks=V(picks), others=V(others))
    outs = dict(
        targets=O((2 * TOPK, size), jnp.int32, 2), columns=O((size, 2 * TOPK), jnp.int32, 2)
    )
    scratch = dict(wide=pltpu.VMEM((128, (size + 127) // 128 * 128), F32))
    return run(body, ins, outs, scratch)


def combine(ns, cfg):
    gather_rows(cfg, ns.mine, ns.ye)
    gather_rows(cfg, ns.theirs, ns.ye, cfg.slots)
    total = ns.hid_in[...]
    for k in range(TOPK):
        table = one_hot(ns.cols_in[:, 2 + k : 3 + k], 2 * cfg.slots).astype(F32).astype(LOW)
        chosen = dot(table, ns.ye[...])
        ns.sel[k] = chosen.astype(LOW)
        total = total + ns.gates_in[:, k : k + 1] * chosen
    return total


def gather_rows(cfg, chunks, target, base=0):
    for c in range(cfg.chunks):
        target[base + c * cfg.rows : base + (c + 1) * cfg.rows, :] = chunks[c][...]


def fetch_halves(first, direct, forwarded, target, sems):
    half = target.shape[0] // 2
    fetch(first, direct, forwarded, target.at[0:half], sems.at[0])
    fetch(first, forwarded, direct, target.at[half:], sems.at[1])


def wait_halves(target, sems):
    half = target.shape[0] // 2
    arrived(target.at[0:half], sems.at[0])
    arrived(target.at[half:], sems.at[1])


def fetch_attention(ns, cfg):
    first = ns.info[0] == 0
    for d in range(cfg.tensor):
        queries, out = [ns.wq_d[d], ns.wq_f[d]], None
        if not ns.joined:
            out = [ns.wo_d[d], ns.wo_f[d]]
        if ns.joined:
            part = 3 * cfg.cols // 2
            out = [ref.at[part:] for ref in queries]
            queries = [ref.at[0:part] for ref in queries]
        fetch_halves(first, *queries, ns.wq.at[d], ns.sem.at[0, d])
        fetch_halves(first, *out, ns.wo.at[d], ns.sem.at[1, d])


def wait_attention(ns, d):
    wait_halves(ns.wq.at[d], ns.sem.at[0, d])
    wait_halves(ns.wo.at[d], ns.sem.at[1, d])


def project(ns, cfg, d, rows):
    cols = cfg.cols
    return [
        dot_nt(rows, ns.wq[d, i * cols : (i + 1) * cols, :]).astype(LOW) for i in range(3)
    ]


def softmax_rows(scores, real):
    scores = jnp.where(real, scores, -1e30)
    largest = jnp.max(scores, axis=-1, keepdims=True)
    shifted = jnp.exp(scores - largest)
    total = jnp.sum(shifted, axis=-1, keepdims=True)
    return shifted / total, largest + jnp.log(total)


def heads_forward(cfg, queries, keys, values):
    head_of = lanes(cfg.cols) // HEAD
    real = lanes(cfg.padded) < cfg.seq
    zero = jnp.zeros((), LOW)
    mixed = jnp.zeros((cfg.padded, cfg.cols), F32)
    logs = []
    for h in range(cfg.heads):
        scores = dot_nt(jnp.where(head_of == h, queries, zero), keys) * HEAD ** (-0.5)
        probs, log = softmax_rows(scores, real)
        mixed = mixed + dot(probs.astype(LOW), jnp.where(head_of == h, values, zero))
        logs.append(log)
    return mixed.astype(LOW), logs


def normed_rows(ns, rows):
    unit, _ = unit_rows(rows)
    return (unit * ns.pack[0:1, :] + ns.pack[1:2, :]).astype(LOW)


def route_rows(ns, cfg):
    unit, _ = unit_rows(ns.hid[...])
    normed = unit * ns.pack[2:3, :] + ns.pack[3:4, :]
    ns.mm[...] = normed.astype(LOW)
    logits = dot_nt(normed, ns.pack[4 : 4 + cfg.experts, :], HIGHEST)
    logits = logits - jnp.max(logits, axis=-1, keepdims=True)
    probs = jnp.exp(logits)
    probs = probs / jnp.sum(probs, axis=-1, keepdims=True)
    ns.probs[...] = probs
    gates = jnp.zeros((cfg.padded, 128), F32)
    for k in range(TOPK):
        hot = one_hot(ns.cols[:, k : k + 1], cfg.experts)
        gate = jnp.sum(jnp.where(hot, probs, 0.0), axis=-1, keepdims=True)
        gates = jnp.where(lanes(128) == k, gate, gates)
    ns.gates[...] = gates


def route_outs(cfg):
    rows, width = cfg.padded, cfg.width
    return dict(
        hid=O((rows, width), F32),
        mm=O((rows, width), LOW),
        probs=O((rows, cfg.experts), F32),
        gates=O((rows, 128), F32),
    )


def attention_flops(cfg):
    return cfg.padded * cfg.width * cfg.width * 8 + 4 * cfg.padded**2 * cfg.width * 4


def attention_heads(cfg, tokens, direct, forwarded, pack):
    def body(ns):
        fetch(ns.info[0] == 0, ns.direct, ns.forwarded, ns.wq.at[0], ns.sem.at[0])
        for d in range(cfg.tensor):
            ns.z[d][0 : cfg.seq, :] = ns.tokens[image_of(ns, d, 0)]
            ns.z[d][cfg.seq :, :] = jnp.zeros((cfg.padded - cfg.seq, cfg.width), LOW)
            ns.a[d] = normed_rows(ns, ns.z[d][...].astype(F32))
        arrived(ns.wq.at[0], ns.sem.at[0])

        def chunk(d, carry):
            ns.mixed[d] = heads_forward(cfg, *project(ns, cfg, 0, ns.a[d]))[0]
            return carry

        lax.fori_loop(0, cfg.tensor, chunk, 0)
        for d in range(cfg.tensor):
            ns.o[d][...] = ns.mixed[d]

    ins = dict(
        info=S(cfg.info),
        order=S(cfg.order),
        tokens=V(tokens),
        direct=A(direct),
        forwarded=A(forwarded),
        pack=V(pack),
    )
    outs = dict(
        o=O((cfg.padded, cfg.cols), LOW, cfg.tensor), z=O((cfg.padded, cfg.width), LOW, cfg.tensor)
    )
    scratch = dict(
        wq=pltpu.VMEM((1, 3 * cfg.cols, cfg.width), LOW),
        a=pltpu.VMEM((cfg.tensor, cfg.padded, cfg.width), LOW),
        mixed=pltpu.VMEM((cfg.tensor, cfg.padded, cfg.cols), LOW),
        sem=pltpu.SemaphoreType.DMA((1,)),
    )
    return run(body, ins, outs, scratch, attention_flops(cfg))


def attention_out(cfg, rows, mixed, weights, pack, cols):
    def body(ns):
        first = ns.info[0] == 0
        for d in range(cfg.tensor):
            fetch_halves(first, ns.wo_d[d], ns.wo_f[d], ns.wo.at[d], ns.sem.at[d])
        total = ns.z[...].astype(F32)
        for d in range(cfg.tensor):
            wait_halves(ns.wo.at[d], ns.sem.at[d])
            total = total + dot(ns.mixed[d][...], ns.wo[d])
        ns.hid[...] = total
        route_rows(ns, cfg)

    ins = dict(
        info=S(cfg.info),
        z=V(rows),
        mixed=V(mixed),
        wo_d=A(weights.wo_d),
        wo_f=A(weights.wo_f),
        pack=V(pack),
        cols=V(cols),
    )
    scratch = dict(
        wo=pltpu.VMEM((cfg.tensor, cfg.cols, cfg.width), LOW),
        sem=pltpu.SemaphoreType.DMA((cfg.tensor, 2)),
    )
    flops = 2 * cfg.padded * cfg.width * cfg.width
    return run(body, ins, route_outs(cfg), scratch, flops)


def combine_ins(mine, theirs, saved, cols):
    return dict(
        mine=V(mine),
        theirs=V(theirs),
        hid_in=V(saved.hid),
        gates_in=V(saved.gates),
        cols_in=V(cols),
    )


def combine_outs(cfg):
    return dict(
        out=O((cfg.padded, cfg.width), LOW), sel=O((TOPK, cfg.padded, cfg.width), LOW)
    )


def combine_attention(cfg, mine, theirs, saved, cols_in, weights, pack, cols):
    def body(ns):
        ns.joined = True
        fetch_attention(ns, cfg)
        ns.out[...] = combine(ns, cfg).astype(LOW)
        rows = ns.out[...].astype(F32)
        ns.a[...] = normed_rows(ns, rows)
        ns.hid[...] = rows
        ns.lse[...] = jnp.zeros_like(ns.lse)

        def chunk(d, carry):
            wait_attention(ns, d)
            parts = project(ns, cfg, d, ns.a[...])
            for i in range(3):
                ns.qkv[d, i] = parts[i]
            mixed, logs = heads_forward(cfg, *parts)
            for h in range(cfg.heads):
                place = lanes(128) == cfg.heads * d + h
                ns.lse[...] = jnp.where(place, logs[h], ns.lse[...])
            ns.mixed[d] = mixed
            ns.hid[...] += dot(mixed, ns.wo[d])
            return carry

        lax.fori_loop(0, cfg.tensor, chunk, 0)
        for d in range(cfg.tensor):
            ns.o[d][...] = ns.mixed[d]
        route_rows(ns, cfg)

    ins = dict(info=S(cfg.info), pack=V(pack), cols=V(cols))
    ins.update(combine_ins(mine, theirs, saved, cols_in))
    ins.update(weights.attention())
    outs = {**combine_outs(cfg), **route_outs(cfg)}
    outs.update(
        qkv=O((cfg.tensor, 3, cfg.padded, cfg.cols), LOW),
        lse=O((cfg.padded, 128), F32),
        o=O((cfg.padded, cfg.cols), LOW, cfg.tensor),
    )
    scratch = dict(
        wq=pltpu.VMEM((cfg.tensor, 3 * cfg.cols, cfg.width), LOW),
        wo=pltpu.VMEM((cfg.tensor, cfg.cols, cfg.width), LOW),
        a=pltpu.VMEM((cfg.padded, cfg.width), LOW),
        mixed=pltpu.VMEM((cfg.tensor, cfg.padded, cfg.cols), LOW),
        ye=pltpu.VMEM((2 * cfg.slots, cfg.width), LOW),
        sem=pltpu.SemaphoreType.DMA((2, cfg.tensor, 2)),
    )
    return run(body, ins, outs, scratch, attention_flops(cfg))


def last_combine(cfg, mine, theirs, saved, cols_in):
    def body(ns):
        ns.out[...] = combine(ns, cfg).astype(LOW)

    scratch = dict(ye=pltpu.VMEM((2 * cfg.slots, cfg.width), LOW))
    flops = 8 * cfg.padded * cfg.slots * cfg.width
    ins = combine_ins(mine, theirs, saved, cols_in)
    return run(body, ins, combine_outs(cfg), scratch, flops)


def slot_rows(ns, cfg, image, choices):
    place = lax.broadcasted_iota(jnp.int32, (cfg.slots, cfg.padded), 0)
    hot = None
    for k in choices:
        row = TOPK * image + k
        here = place == ns.targets[row : row + 1, :]
        hot = here if hot is None else hot | here
    return hot.astype(F32).astype(LOW)


def send_rows(ns, cfg, rows):
    for c in range(cfg.chunks):
        ns.sent[c][...] = rows[c * cfg.rows : (c + 1) * cfg.rows, :]


def dispatch(cfg, mine, theirs, targets):
    def body(ns):
        rows = dot(slot_rows(ns, cfg, 0, range(TOPK)), ns.mine[...])
        rows = rows + dot(slot_rows(ns, cfg, 1, range(TOPK)), ns.theirs[...])
        send_rows(ns, cfg, rows.astype(LOW))

    ins = dict(mine=V(mine), theirs=V(theirs), targets=V(targets))
    outs = dict(sent=O((cfg.rows, cfg.width), LOW, cfg.chunks))
    return run(body, ins, outs, None, 4 * cfg.slots * cfg.padded * cfg.width).sent


def dispatch_back(cfg, mine, theirs, gates_mine, gates_theirs, targets):
    whole = theirs is None

    def body(ns):
        if whole:
            grads = (ns.rows, ns.other)
            for i, grad in enumerate(grads):
                grad[0 : cfg.seq, :] = ns.mine[image_of(ns, 0, i)]
                grad[cfg.seq :, :] = jnp.zeros((cfg.padded - cfg.seq, cfg.width), LOW)
        else:
            grads = (ns.mine, ns.theirs)
        rows = jnp.zeros((cfg.slots, cfg.width), F32)
        for image, (grad, gates) in enumerate(zip(grads, (ns.gates_mine, ns.gates_theirs))):
            for k in range(TOPK):
                weighted = (gates[:, k : k + 1] * grad[...].astype(F32)).astype(LOW)
                rows = rows + dot(slot_rows(ns, cfg, image, (k,)), weighted)
        send_rows(ns, cfg, rows.astype(LOW))

    ins = dict(
        mine=V(mine),
        gates_mine=V(gates_mine),
        gates_theirs=V(gates_theirs),
        targets=V(targets),
        info=S(cfg.info),
    )
    outs = dict(sent=O((cfg.rows, cfg.width), LOW, cfg.chunks))
    scratch = None
    if whole:
        ins.update(order=S(cfg.order))
        outs.update(rows=O((cfg.padded, cfg.width), LOW))
        scratch = dict(other=pltpu.VMEM((cfg.padded, cfg.width), LOW))
    else:
        ins.update(theirs=V(theirs))
    flops = 8 * cfg.slots * cfg.padded * cfg.width
    return run(body, ins, outs, scratch, flops)


TILE = 256


def fetch_experts(ns, d, matrix):
    first = ns.info[0] == 0
    if matrix == 0:
        fetch(first, ns.we_d[d], ns.we_f[d], ns.wi.at[d], ns.sem.at[0, d])
    else:
        fetch(first, ns.we_f[d], ns.we_d[d], ns.wb.at[d], ns.sem.at[1, d])


def expert_scratch(cfg):
    return dict(
        wi=pltpu.VMEM((cfg.tensor, cfg.width, cfg.hidden), LOW),
        wb=pltpu.VMEM((cfg.tensor, cfg.hidden, cfg.width), LOW),
        acc=pltpu.VMEM((cfg.slots, cfg.width), F32),
        sem=pltpu.SemaphoreType.DMA((3, cfg.tensor)),
        out_sem=pltpu.SemaphoreType.DMA((2, cfg.tensor)),
    )


def expert_flops(cfg):
    return 4 * cfg.slots * cfg.width * cfg.hidden * cfg.tensor


def experts_forward(cfg, chunks, weights):
    def body(ns):
        for d in range(cfg.tensor):
            fetch_experts(ns, d, 0)
            fetch_experts(ns, d, 1)
        gather_rows(cfg, ns.chunks, ns.x)
        ns.acc[...] = jnp.zeros_like(ns.acc)

        def chunk(d, carry):
            arrived(ns.wi.at[d], ns.sem.at[0, d])
            for place in range(0, cfg.slots, TILE):
                part = slice(place, place + TILE)
                act, slope = gelu_pair(dot(ns.x[part, :], ns.wi[d]))
                ns.act_s[d, part, :] = act.astype(LOW)
                ns.slope_s[d, part, :] = slope.astype(LOW)
            arrived(ns.wb.at[d], ns.sem.at[1, d])
            ns.acc[...] += dot(ns.act_s[d], ns.wb[d])
            pltpu.make_async_copy(ns.act_s.at[d], ns.act.at[d], ns.out_sem.at[0, d]).start()
            pltpu.make_async_copy(ns.slope_s.at[d], ns.slope.at[d], ns.out_sem.at[1, d]).start()
            return carry

        lax.fori_loop(0, cfg.tensor, chunk, 0)
        for c in range(cfg.chunks):
            ns.ye[c][...] = ns.acc[c * cfg.rows : (c + 1) * cfg.rows, :].astype(LOW)
        for d in range(cfg.tensor):
            arrived(ns.act_s.at[d], ns.out_sem.at[0, d])
            arrived(ns.slope_s.at[d], ns.out_sem.at[1, d])

    ins = dict(info=S(cfg.info), chunks=V(chunks), **weights.experts())
    hidden = (cfg.tensor, cfg.slots, cfg.hidden)
    outs = dict(
        x=O((cfg.slots, cfg.width), LOW),
        ye=O((cfg.rows, cfg.width), LOW, cfg.chunks),
        act=O(hidden, LOW, space=pl.ANY),
        slope=O(hidden, LOW, space=pl.ANY),
    )
    scratch = dict(
        act_s=pltpu.VMEM(hidden, LOW), slope_s=pltpu.VMEM(hidden, LOW), **expert_scratch(cfg)
    )
    return run(body, ins, outs, scratch, expert_flops(cfg))


def experts_back(cfg, chunks, rows, act, slope, weights):
    def body(ns):
        first = ns.info[0] == 0
        for d in range(cfg.tensor):
            fetch_experts(ns, d, 1)
            pltpu.make_async_copy(ns.slope.at[d], ns.slope_s.at[d], ns.sem.at[2, d]).start()
            fetch_experts(ns, d, 0)

            @pl.when(first)
            def _():
                pltpu.make_async_copy(ns.act.at[d], ns.act_s.at[d], ns.act_sem.at[d]).start()

        gather_rows(cfg, ns.chunks, ns.x)
        ns.acc[...] = jnp.zeros_like(ns.acc)

        def chunk(d, carry):
            arrived(ns.wb.at[d], ns.sem.at[1, d])
            arrived(ns.slope_s.at[d], ns.sem.at[2, d])
            arrived(ns.wi.at[d], ns.sem.at[0, d])
            for place in range(0, cfg.slots, TILE):
                part = slice(place, place + TILE)
                grad = dot_nt(ns.x[part, :], ns.wb[d]) * ns.slope_s[d, part, :].astype(F32)
                grad = grad.astype(LOW)
                ns.dpre_s[d, part, :] = grad
                ns.acc[part, :] += dot_nt(grad, ns.wi[d])
            pltpu.make_async_copy(ns.dpre_s.at[d], ns.dpre.at[d], ns.out_sem.at[0, d]).start()

            @pl.when(first)
            def _():
                arrived(ns.act_s.at[d], ns.act_sem.at[d])

            fetch(first, ns.act_s.at[d], ns.dpre_s.at[d], ns.hidden.at[d], ns.out_sem.at[1, d])
            return carry

        lax.fori_loop(0, cfg.tensor, chunk, 0)
        ns.rows_out[...] = jnp.where(first, ns.x[...].astype(F32), ns.rows[...].astype(F32)).astype(LOW)
        for c in range(cfg.chunks):
            ns.dxe[c][...] = ns.acc[c * cfg.rows : (c + 1) * cfg.rows, :].astype(LOW)
        for d in range(cfg.tensor):
            arrived(ns.dpre_s.at[d], ns.out_sem.at[0, d])
            arrived(ns.dpre_s.at[d], ns.out_sem.at[1, d])

    ins = dict(
        info=S(cfg.info),
        chunks=V(chunks),
        rows=V(rows),
        act=A(act),
        slope=A(slope),
        **weights.experts(),
    )
    hidden = (cfg.tensor, cfg.slots, cfg.hidden)
    outs = dict(
        x=O((cfg.slots, cfg.width), LOW),
        dxe=O((cfg.rows, cfg.width), LOW, cfg.chunks),
        dpre=O(hidden, LOW, space=pl.ANY),
        rows_out=O((cfg.slots, cfg.width), LOW),
        hidden=O(hidden, LOW, space=pl.ANY),
    )
    scratch = dict(
        dpre_s=pltpu.VMEM(hidden, LOW),
        slope_s=pltpu.VMEM(hidden, LOW),
        act_s=pltpu.VMEM(hidden, LOW),
        act_sem=pltpu.SemaphoreType.DMA((cfg.tensor,)),
        **expert_scratch(cfg),
    )
    return run(body, ins, outs, scratch, expert_flops(cfg))


def experts_grads(cfg, xe, dye, act, dpre, rows, hidden):
    size = cfg.slots

    def body(ns):
        first = ns.info[0] == 0
        fetch(first, ns.xe, ns.dye, ns.fixed.at[0:size], ns.fixed_sem.at[0])
        pltpu.make_async_copy(ns.rows, ns.fixed.at[size:], ns.fixed_sem.at[1]).start()
        for d in range(cfg.tensor):
            fetch(first, ns.dpre.at[d], ns.act.at[d], ns.moving.at[d, 0:size], ns.sem.at[0, d])
            pltpu.make_async_copy(
                ns.hidden.at[d], ns.moving.at[d, size:], ns.sem.at[1, d]
            ).start()
        arrived(ns.fixed.at[0:size], ns.fixed_sem.at[0])
        arrived(ns.fixed.at[size:], ns.fixed_sem.at[1])
        ns.turned[...] = ns.fixed[...].T

        def chunk(d, carry):
            arrived(ns.moving.at[d, 0:size], ns.sem.at[0, d])
            arrived(ns.moving.at[d, size:], ns.sem.at[1, d])
            ns.out_s[d] = dot(ns.turned[...], ns.moving[d]).astype(LOW)
            for k in range(cfg.tensor):

                @pl.when(d == k)
                def _():
                    pltpu.make_async_copy(ns.out_s.at[k], ns.out[k], ns.out_sem.at[k]).start()

            return carry

        lax.fori_loop(0, cfg.tensor, chunk, 0)
        for d in range(cfg.tensor):
            arrived(ns.out_s.at[d], ns.out_sem.at[d])

    ins = dict(
        info=S(cfg.info),
        xe=A(xe),
        dye=A(dye),
        act=A(act),
        dpre=A(dpre),
        rows=A(rows),
        hidden=A(hidden),
    )
    shape = (cfg.width, cfg.hidden)
    outs = dict(out=O(shape, LOW, cfg.tensor, space=pl.ANY))
    scratch = dict(
        fixed=pltpu.VMEM((2 * size, cfg.width), LOW),
        turned=pltpu.VMEM((cfg.width, 2 * size), LOW),
        moving=pltpu.VMEM((cfg.tensor, 2 * size, cfg.hidden), LOW),
        out_s=pltpu.VMEM((cfg.tensor,) + shape, LOW),
        fixed_sem=pltpu.SemaphoreType.DMA((2,)),
        sem=pltpu.SemaphoreType.DMA((2, cfg.tensor)),
        out_sem=pltpu.SemaphoreType.DMA((cfg.tensor,)),
    )
    return run(body, ins, outs, scratch, expert_flops(cfg)).out


def back_to_attention(cfg, grad, saved, sel, mine, theirs, pack, cols):
    def body(ns):
        gather_rows(cfg, ns.mine, ns.dx)
        gather_rows(cfg, ns.theirs, ns.dx, cfg.slots)
        grad = ns.grad[...].astype(F32)
        grad_probs = jnp.zeros((cfg.padded, cfg.experts), F32)
        hot = None
        for k in range(TOPK):
            grad_gate = jnp.sum(grad * ns.sel[k].astype(F32), axis=-1, keepdims=True)
            route = one_hot(ns.cols[:, k : k + 1], cfg.experts)
            grad_probs = grad_probs + jnp.where(route, grad_gate, 0.0)
            place = one_hot(ns.cols[:, 2 + k : 3 + k], 2 * cfg.slots)
            hot = place if hot is None else hot | place
        probs = ns.probs[...]
        grad_logits = probs * (
            grad_probs - jnp.sum(probs * grad_probs, axis=-1, keepdims=True)
        )
        grad_norm = dot(hot.astype(F32).astype(LOW), ns.dx[...])
        grad_norm = grad_norm + dot(grad_logits, ns.pack[4 : 4 + cfg.experts, :], HIGHEST)
        unit, inverse = unit_rows(ns.hid[...])
        gain = ns.pack[2:3, :]
        normed = unit * gain + ns.pack[3:4, :]
        e = cfg.experts
        ns.small[...] = jnp.zeros_like(ns.small)
        ns.small[0:e, :] = dot_tn(grad_logits, normed, HIGHEST)
        ns.small[e : e + 1, :] = jnp.sum(grad_norm * unit, axis=0, keepdims=True)
        ns.small[e + 1 : e + 2, :] = jnp.sum(grad_norm, axis=0, keepdims=True)
        grad_hidden = grad + norm_back(grad_norm, unit, inverse, gain)
        ns.dh[...] = grad_hidden
        ns.datt[0 : cfg.padded, :] = grad_hidden.astype(LOW)
        ns.datt[cfg.padded :, :] = ns.small[...].astype(LOW)

    ins = dict(
        grad=V(grad),
        sel=V(sel),
        mine=V(mine),
        theirs=V(theirs),
        hid=V(saved.hid),
        probs=V(saved.probs),
        pack=V(pack),
        cols=V(cols),
    )
    outs = dict(
        dh=O((cfg.padded, cfg.width), F32),
        datt=O((cfg.padded + cfg.small, cfg.width), LOW),
    )
    scratch = dict(
        dx=pltpu.VMEM((2 * cfg.slots, cfg.width), LOW),
        small=pltpu.VMEM((cfg.small, cfg.width), F32),
    )
    flops = 4 * cfg.padded * cfg.slots * cfg.width
    return run(body, ins, outs, scratch, flops)


def attention_back(cfg, rows, saved, back, weights, pack, again):
    def body(ns):
        ns.joined = not again
        fetch_attention(ns, cfg)
        cols = cfg.cols
        head_of = lanes(cols) // HEAD
        real = lanes(cfg.padded) < cfg.seq
        zero = jnp.zeros((), LOW)
        ns.acc[...] = jnp.zeros_like(ns.acc)
        if again:
            ns.a[...] = normed_rows(ns, ns.z[...].astype(F32))

        def chunk(d, carry):
            wait_attention(ns, d)
            grad_mixed = dot_nt(ns.datt[0 : cfg.padded, :], ns.wo[d]).astype(LOW)
            if again:
                queries, keys, values = project(ns, cfg, d, ns.a[...])
            else:
                queries, keys, values = ns.qkv[d, 0], ns.qkv[d, 1], ns.qkv[d, 2]
            grad_q = jnp.zeros((cfg.padded, cols), F32)
            grad_k, grad_v = grad_q, grad_q
            for h in range(cfg.heads):
                mine = head_of == h
                query = jnp.where(mine, queries, zero)
                grad_head = jnp.where(mine, grad_mixed, zero)
                scores = dot_nt(query, keys) * HEAD ** (-0.5)
                if again:
                    probs, _ = softmax_rows(scores, real)
                else:
                    place = lanes(128) == cfg.heads * d + h
                    lse = jnp.sum(jnp.where(place, ns.lse[...], 0.0), axis=-1, keepdims=True)
                    probs = jnp.exp(jnp.where(real, scores - lse, -1e30))
                grad_v = grad_v + dot_tn(probs.astype(LOW), grad_head)
                grad_probs = dot_nt(grad_head, values)
                inner = jnp.sum(probs * grad_probs, axis=-1, keepdims=True)
                grad_scores = (probs * (grad_probs - inner)).astype(LOW)
                grad_q = grad_q + dot(grad_scores, jnp.where(mine, keys, zero))
                grad_k = grad_k + dot_tn(grad_scores, query)
            grads = (grad_q * HEAD ** (-0.5), grad_k * HEAD ** (-0.5), grad_v)
            total = ns.acc[...]
            for i, grad in enumerate(grads):
                grad = grad.astype(LOW)
                ns.grads[d, i] = grad
                total = total + dot(grad, ns.wq[d, i * cols : (i + 1) * cols, :])
            ns.acc[...] = total
            return carry

        lax.fori_loop(0, cfg.tensor, chunk, 0)
        unit, inverse = unit_rows(ns.z[...].astype(F32))
        grad = ns.acc[...]
        dz = (ns.dh[...] + norm_back(grad, unit, inverse, ns.pack[0:1, :])).astype(LOW)
        ns.dz[...] = dz
        ns.small[...] = jnp.zeros_like(ns.small)
        ns.small[0:1, :] = jnp.sum(grad * unit, axis=0, keepdims=True)
        ns.small[1:2, :] = jnp.sum(grad, axis=0, keepdims=True)
        small = ns.small[...].astype(LOW)
        rows = cfg.padded
        for d in range(cfg.tensor):
            for i in range(3):
                ns.sent[d][0:rows, i * cols : (i + 1) * cols] = ns.grads[d, i]
            if again:
                ns.sent[d][rows : rows + 16, :] = small[:, 0 : 3 * cols]
                ns.sent[d][rows + 16 :, 0:cols] = small[:, 3 * cols :]
            else:
                ns.sent[d][:, 3 * cols :] = ns.o[d][...]
        if not again:
            width, end = cfg.width, rows + cfg.small
            ns.common[0:end, 0:width] = ns.datt[...]
            ns.common[end:, 0:width] = small
            ns.common[0:rows, width:] = dz

    ins = dict(
        info=S(cfg.info),
        z=V(rows),
        pack=V(pack),
        datt=V(back.datt),
        dh=V(back.dh),
        **weights.attention(),
    )
    scratch = dict(
        wq=pltpu.VMEM((cfg.tensor, 3 * cfg.cols, cfg.width), LOW),
        wo=pltpu.VMEM((cfg.tensor, cfg.cols, cfg.width), LOW),
        acc=pltpu.VMEM((cfg.padded, cfg.width), F32),
        grads=pltpu.VMEM((cfg.tensor, 3, cfg.padded, cfg.cols), LOW),
        sem=pltpu.SemaphoreType.DMA((2, cfg.tensor, 2)),
    )
    if again:
        scratch.update(a=pltpu.VMEM((cfg.padded, cfg.width), LOW))
    else:
        ins.update(qkv=V(saved.qkv), lse=V(saved.lse), o=V(saved.o))
    scratch.update(small=pltpu.VMEM((16, cfg.width), F32))
    shape = (cfg.padded + 32, 3 * cfg.cols)
    outs = dict(dz=O((cfg.padded, cfg.width), LOW))
    if not again:
        shape = (cfg.padded, cfg.width)
        outs.update(common=O((cfg.padded + cfg.small + 16, 2 * cfg.width), LOW))
    outs.update(sent=O(shape, LOW, cfg.tensor))
    return run(body, ins, outs, scratch, 2 * attention_flops(cfg))


def pair_sum(values):
    while len(values) > 1:
        values = [a + b for a, b in zip(values[::2], values[1::2])]
    return values[0]


def attention_grads(cfg, rows, sent, datt, mixed, pack):
    joined = mixed is None
    cols, width, padded, small = cfg.cols, cfg.width, cfg.padded, cfg.small

    def body(ns):
        first = ns.info[0] == 0
        upper, lower = [], []
        for d in range(cfg.tensor):
            part = slice(d * padded, (d + 1) * padded)
            ns.a[part, :] = normed_rows(ns, ns.rows[d][...].astype(F32))
            ns.g[part, :] = ns.sent[d][0:padded, 0 : 3 * cols]
            ns.t[part, :] = ns.datt[d][0:padded, 0:width]
            upper.append(ns.datt[d][padded : padded + small, 0:width].astype(F32))
            if joined:
                ns.m[part, :] = ns.sent[d][0:padded, 3 * cols : width]
                lower.append(ns.datt[d][padded + small :, 0:width].astype(F32))
            else:
                ns.m[part, :] = ns.mixed[d][...]
                left = ns.sent[d][padded : padded + 16, :].astype(F32)
                right = ns.sent[d][padded + 16 :, 0:cols].astype(F32)
                lower.append(jnp.concatenate([left, right], axis=1))
        ns.acc[0 : 3 * cols, :] = dot_tn(ns.g[...], ns.a[...])
        ns.acc[3 * cols :, :] = dot_tn(ns.m[...], ns.t[...])
        low, high = ns.acc[0 : 2 * cols, :], ns.acc[2 * cols :, :]
        rest = 2 * cols
        ns.keep[0:rest, :] = jnp.where(first, low, high)
        ns.send[0:rest, :] = jnp.where(first, high, low).astype(LOW)
        upper, lower = pair_sum(upper), pair_sum(lower)
        ns.keep[rest : rest + small, :] = upper
        ns.keep[rest + small :, :] = lower
        ns.send[rest : rest + small, :] = upper.astype(LOW)
        ns.send[rest + small :, :] = lower.astype(LOW)

    ins = dict(info=S(cfg.info), rows=V(rows), sent=V(sent), datt=V(datt), pack=V(pack))
    if not joined:
        ins.update(mixed=V(mixed))
    shape = (2 * cols + small + 16, width)
    outs = dict(keep=O(shape, F32), send=O(shape, LOW))
    every = cfg.tensor * padded
    scratch = dict(
        a=pltpu.VMEM((every, width), LOW),
        g=pltpu.VMEM((every, 3 * cols), LOW),
        t=pltpu.VMEM((every, width), LOW),
        m=pltpu.VMEM((every, cols), LOW),
        acc=pltpu.VMEM((4 * cols, width), F32),
    )
    flops = 8 * cfg.tensor * padded * width * cols
    return run(body, ins, outs, scratch, flops)


def split_owners(cfg, keeps, received):
    part, rest = 2 * cfg.cols // cfg.owners, 2 * cfg.cols

    def body(ns):
        for layer in range(2):
            ns.total[...] = ns.keep[layer][...] + ns.received[layer][...].astype(F32)
            for z in range(cfg.owners):
                place = pl.multiple_of((ns.info[1] ^ z) * part, 8)
                ns.pieces[z][layer, 0:part, :] = ns.total[pl.ds(place, part), :].astype(LOW)
                ns.pieces[z][layer, part:, :] = ns.total[rest:, :].astype(LOW)

    ins = dict(info=S(cfg.info), keep=V(keeps), received=V(received))
    outs = dict(pieces=O((2, part + cfg.small + 16, cfg.width), LOW, cfg.owners))
    scratch = dict(total=pltpu.VMEM(keeps[0].shape, F32))
    return run(body, ins, outs, scratch).pieces


def sum_pieces(cfg, pieces):
    part = 2 * cfg.cols // cfg.owners

    def body(ns):
        total = pair_sum([piece[...].astype(F32) for piece in ns.pieces])
        ns.total[...] = total[:, 0:part, :].astype(LOW)
        ns.small[...] = total[:, part:, :]

    outs = dict(
        total=O((2, part, cfg.width), LOW), small=O((2, cfg.small + 16, cfg.width), F32)
    )
    return run(body, dict(pieces=V(pieces)), outs)


def order_attention_grads(cfg, pieces, small):
    part = 2 * cfg.cols // cfg.owners

    def body(ns):
        def place_layer(mine):
            for z in range(cfg.owners):
                place = pl.ds(pl.multiple_of((ns.info[1] ^ z) * part, 8), part)
                ns.own_s[place, :] = ns.pieces[z][mine].astype(F32)
                ns.send_s[place, :] = ns.pieces[z][1 - mine].astype(F32)
            ns.out[...] = ns.small[mine]

        pl.when(ns.info[0] == 0)(lambda: place_layer(0))
        pl.when(ns.info[0] == 1)(lambda: place_layer(1))
        ns.own[...] = ns.own_s[...].astype(LOW)
        ns.send[...] = ns.send_s[...].astype(LOW)

    ins = dict(info=S(cfg.info), pieces=V(pieces), small=V(small))
    shape = (2 * cfg.cols, cfg.width)
    outs = dict(own=O(shape, LOW), send=O(shape, LOW), out=O(small.shape[1:], F32))
    scratch = dict(own_s=pltpu.VMEM(shape, F32), send_s=pltpu.VMEM(shape, F32))
    return run(body, ins, outs, scratch)


def place_attention_grads(cfg, own, received):
    cols = cfg.cols

    def body(ns):
        first = ns.info[0] == 0
        low = jnp.where(first, ns.own[...].astype(F32), ns.received[...].astype(F32))
        high = jnp.where(first, ns.received[...].astype(F32), ns.own[...].astype(F32))
        ns.qkv[0, 0] = low[0:cols, :]
        ns.qkv[0, 1] = low[cols:, :]
        ns.qkv[0, 2] = high[0:cols, :]
        ns.out[0] = high[cols:, :]

    ins = dict(info=S(cfg.info), own=V(own), received=V(received))
    outs = dict(qkv=O((1, 3, cols, cfg.width), F32), out=O((1, cols, cfg.width), F32))
    return run(body, ins, outs)


def place_expert_grads(cfg, mine, theirs):
    def body(ns):
        sources = ((ns.mine0, ns.theirs0), (ns.mine1, ns.theirs1))
        for layer in range(2):

            @pl.when(ns.info[0] == layer)
            def _():
                for i in range(2):
                    for j in range(2):
                        matrix = j if layer == 0 else 1 - j
                        pltpu.make_async_copy(
                            sources[layer][j][i], ns.held.at[matrix, i], ns.sem.at[matrix, i]
                        ).start()

        for i in range(2):
            expert = ns.info[3] ^ i
            arrived(ns.held.at[0, i], ns.sem.at[0, i])
            ns.grad_in[0, expert] = ns.held[0, i].astype(F32)
            arrived(ns.held.at[1, i], ns.sem.at[1, i])
            ns.grad_back[0, expert] = ns.held[1, i].T.astype(F32)

    ins = dict(
        info=S(cfg.info),
        mine0=A(mine[0]),
        mine1=A(mine[1]),
        theirs0=A(theirs[0]),
        theirs1=A(theirs[1]),
    )
    outs = dict(
        grad_in=O((1, 2, cfg.width, cfg.hidden), F32),
        grad_back=O((1, 2, cfg.hidden, cfg.width), F32),
    )
    scratch = dict(
        held=pltpu.VMEM((2, 2, cfg.width, cfg.hidden), LOW),
        sem=pltpu.SemaphoreType.DMA((2, 2)),
    )
    return run(body, ins, outs, scratch)


def stack_images(values, place):
    low, high, left, right = place

    def body(ns):
        for d, value in enumerate(ns.values):
            ns.out[d] = value[low:high, left:right]

    outs = dict(out=O((len(values), high - low, right - left), LOW))
    return run(body, dict(values=V(values)), outs).out


def place_images(cfg, mine, theirs, lefts, dtype):
    def body(ns):
        def place_layer(own, other, left):
            for d in range(cfg.tensor):
                image = own[d][0 : cfg.seq, left : left + cfg.width]
                ns.images[0, image_of(ns, d, 0)] = image.astype(dtype)
                ns.images[0, image_of(ns, d, 1)] = other[d, 0 : cfg.seq, :].astype(dtype)

        pl.when(ns.info[0] == 0)(lambda: place_layer(ns.mine0, ns.theirs0, lefts[0]))
        pl.when(ns.info[0] == 1)(lambda: place_layer(ns.mine1, ns.theirs1, lefts[1]))

    ins = dict(
        info=S(cfg.info),
        order=S(cfg.order),
        mine0=V(mine[0]),
        mine1=V(mine[1]),
        theirs0=V(theirs[0]),
        theirs1=V(theirs[1]),
    )
    outs = dict(images=O((1, 2 * cfg.tensor, cfg.seq, cfg.width), dtype))
    return run(body, ins, outs).images


def exchange(cfg, chunks):
    return [
        value if c == 0 else hop(value, *divmod(c, cfg.local))
        for c, value in enumerate(chunks)
    ]


def swaps(chunks):
    return [swap(v) for v in chunks]


def forward_chunks(chunks):
    return swaps(chunks[:3]) + swaps(chunks[3:])


def gather_images(value):
    return [value] + [across(value, d) for d in (1, 2, 3)]


def relay_images(value):
    two = across(value, 2)
    one = across(value, 1)
    three = across(two, 1)
    return [value, one, two, three]


def spread(chunks):
    return [chunks[0]] + [across(chunks[d], d) for d in range(1, len(chunks))]


def relay(own, other):
    one = across(other, 1)
    two = across(own, 2)
    three = across(one, 2)
    return [own, one, two, three]


class Weights:
    wo_d = None

    def attention(self):
        parts = dict(wq_d=A(self.wq_d), wq_f=A(self.wq_f))
        if self.wo_d is not None:
            parts.update(wo_d=A(self.wo_d), wo_f=A(self.wo_f))
        return parts

    def experts(self):
        return dict(we_d=A(self.we_d), we_f=A(self.we_f))


def add(left, right):
    return (left.astype(F32) + right.astype(F32)).astype(LOW)


def program(
    tokens,
    batch_order,
    gain_attn,
    shift_attn,
    w_qkv,
    w_out,
    gain_moe,
    shift_moe,
    w_router,
    w_in,
    w_back,
    routes,
    slots,
    cotangent,
):
    section, expert, tensor = (lax.axis_index(n) for n in (SECTION, EXPERT, TENSOR))
    owners, count = lax.axis_size(EXPERT), lax.axis_size(TENSOR)
    local = w_in.shape[1]
    seq, width = tokens.shape[1], tokens.shape[2]
    experts = local * owners
    capacity = (TOPK * IMG_MB * seq * 5 // (4 * experts) + 7) // 8 * 8
    padded = (seq + 15) // 16 * 16
    small = (experts + 2 + 15) // 16 * 16
    cfg = SimpleNamespace(
        tensor=count,
        owners=owners,
        local=local,
        experts=experts,
        seq=seq,
        width=width,
        padded=padded,
        small=small,
        cols=w_qkv.shape[3],
        heads=w_qkv.shape[3] // HEAD,
        hidden=w_in.shape[3],
        chunks=owners * local,
        rows=capacity // 2,
        slots=owners * local * capacity // 2,
    )
    assert count == MB == 4 and local == 2 and IMG_MB == 2 and cfg.width == cfg.hidden
    local_expert = tensor % local
    cfg.info = jnp.stack([section, expert, tensor, local_expert]).astype(jnp.int32)
    cfg.order = batch_order[0]
    first_core = section == 0
    wq = w_qkv[0].transpose(0, 2, 1).reshape(3 * cfg.cols, width)
    wo = w_out[0]
    wq_half, wo_half = 3 * cfg.cols // 2, cfg.cols // 2
    sibling_wq = to_sibling(wq, 0)
    pack = jnp.concatenate([gain_attn, shift_attn, gain_moe, shift_moe, w_router[0].T], axis=0)
    other_pack = swap(pack)
    packs = [
        jnp.where(first_core, pack, other_pack),
        jnp.where(first_core, other_pack, pack),
    ]
    picks = jnp.stack(
        [v[0].reshape(MB, IMG_MB, seq, TOPK)[tensor] for v in (routes, slots)]
    ).transpose(0, 1, 3, 2)
    picks = jnp.pad(picks, ((0, 0), (0, 0), (0, 0), (0, padded - seq)), constant_values=-1)
    picks = picks.reshape(4 * TOPK, padded)
    planned = plan(cfg, picks, swap(picks))
    targets, columns = planned.targets, planned.columns

    def pick(values, index):
        return lax.dynamic_index_in_dim(values, index, 0, keepdims=False)

    weights = [Weights(), Weights()]
    sibling_wo = to_sibling(wo[wo_half:], 0)
    sibling_we = to_sibling(w_back[0], 0)
    wo_own = jnp.where(first_core, wo[:wo_half], sibling_wo)
    weights[0].wo_d = gather_images(wo_own)
    weights[0].wo_f = swaps(weights[0].wo_d)

    def pair(lower, upper):
        return [
            jnp.where(first_core, pick(lower, index), pick(upper, index))
            for index in (local_expert, 1 - local_expert)
        ]

    first_pair = pair(w_in[0], sibling_we)
    weights[0].we_d = relay(*first_pair)
    weights[0].we_f = forward_chunks(weights[0].we_d)
    joined = [jnp.concatenate([wq[:wq_half], wo[:wo_half]], axis=0)]
    joined.append(jnp.concatenate([wq[wq_half:], wo[wo_half:]], axis=0))
    joined = jnp.where(first_core, to_owner(joined[0], 0), joined[1])
    weights[1].wq_d = relay(joined, joined)
    weights[1].wq_f = swaps(weights[1].wq_d)
    sibling_we = to_owner(w_in[0], 0)
    weights[1].we_d = relay(*pair(sibling_we, w_back[0]))
    weights[1].we_f = forward_chunks(weights[1].we_d)
    wq0_own = jnp.where(first_core, wq[:wq_half], sibling_wq[wq_half:])
    weights[0].wq_d = gather_images(wq0_own)
    weights[0].wq_f = swaps(weights[0].wq_d)

    tokens = lax.optimization_barrier((tokens, *first_pair))[0]
    heads = attention_heads(cfg, tokens, wq, sibling_wq, packs[0])
    rows, saved, arrived_rows, forward = [heads.z], [], [], []
    first = attention_out(cfg, heads.z[0], spread(heads.o), weights[0], packs[0], columns[0])
    saved.append(first)
    sent = dispatch(cfg, first.mm, swap(first.mm), targets[0])
    arrived_rows.append(exchange(cfg, sent))
    other_gates = [swap(first.gates)]
    forward.append(experts_forward(cfg, arrived_rows[0], weights[0]))
    mine = exchange(cfg, forward[0].ye)
    second = combine_attention(
        cfg, mine, swaps(mine), first, columns[0], weights[1], packs[1], columns[1]
    )
    saved.append(second)
    other_gates.append(swap(second.gates))
    rows.append(gather_images(second.out))
    sent = dispatch(cfg, second.mm, swap(second.mm), targets[1])
    arrived_rows.append(exchange(cfg, sent))
    sent = dispatch_back(cfg, cotangent, None, second.gates, other_gates[1], targets[1])
    target_rows = sent.rows
    arrived_grads = [None, exchange(cfg, sent.sent)]
    forward.append(experts_forward(cfg, arrived_rows[1], weights[1]))
    mine = exchange(cfg, forward[1].ye)
    final = last_combine(cfg, mine, swaps(mine), second, columns[1])
    last_rows = relay_images(final.out)
    selected = [second.sel, final.sel]

    grad_rows = [None, None, target_rows]
    expert_grads, parts = [None, None], [None, None]
    for layer in (1, 0):
        if layer == 0:
            sent = dispatch_back(
                cfg, grad_rows[1], swap(grad_rows[1]), first.gates, other_gates[0], targets[0]
            )
            arrived_grads[0] = exchange(cfg, sent.sent)
        back = experts_back(
            cfg,
            arrived_grads[layer],
            forward[layer].x,
            forward[layer].act,
            forward[layer].slope,
            weights[layer],
        )
        mine = exchange(cfg, back.dxe)
        zero, one, two, three = experts_grads(
            cfg,
            forward[layer].x,
            back.x,
            forward[layer].act,
            back.dpre,
            swap(back.rows_out),
            swap(back.hidden),
        )
        three = across(three, 2)
        two = across(two, 2)
        one = add(one, three)
        one = across(one, 1)
        own = add(zero, two)
        expert_grads[layer] = (
            [own, one],
            [to_owner(own, layer), to_owner(one, layer)],
        )
        upper = back_to_attention(
            cfg,
            grad_rows[layer + 1],
            saved[layer],
            selected[layer],
            mine,
            swaps(mine),
            packs[layer],
            columns[layer],
        )
        datt = gather_images(upper.datt) if layer == 0 else None
        lower = attention_back(
            cfg, rows[layer][0], saved[layer], upper, weights[layer], packs[layer], layer == 0
        )
        grad_rows[layer] = lower.dz
        sent = spread(lower.sent)
        if layer == 1:
            datt = last_common = relay_images(lower.common)
        grads = attention_grads(
            cfg, rows[layer], sent, datt, heads.o if layer == 0 else None, packs[layer]
        )
        parts[layer] = grads.keep, swap(grads.send)

    split = split_owners(cfg, *zip(*parts))
    split = [split[0]] + [along(split[z], z) for z in range(1, owners)]
    piece = sum_pieces(cfg, split)
    pieces = [piece.total] + [along(piece.total, z) for z in range(1, owners)]

    image = (0, padded, 0, width)
    stacks = [
        to_owner(stack_images(rows[1], image), 0), to_owner(stack_images(last_rows, image), 1)
    ]
    acts = place_images(cfg, [rows[1], last_rows], stacks, (0, 0), LOW)
    first_grads = relay_images(grad_rows[0])
    stacks = [
        to_owner(stack_images(first_grads, image), 0),
        to_owner(stack_images(last_common, (0, padded, width, 2 * width)), 1),
    ]
    in_grads = place_images(cfg, [first_grads, last_common], stacks, (0, width), LOW).astype(F32)
    ordered = order_attention_grads(cfg, pieces, piece.small)
    attention_final = place_attention_grads(cfg, ordered.own, swap(ordered.send))
    final_small = ordered.out
    expert_final = place_expert_grads(cfg, *zip(*expert_grads))
    return (
        acts,
        in_grads,
        final_small[small][None],
        final_small[small + 1][None],
        attention_final.qkv.transpose(0, 1, 3, 2),
        attention_final.out,
        final_small[experts][None],
        final_small[experts + 1][None],
        final_small[:experts].T[None],
        expert_final.grad_in,
        expert_final.grad_back,
    )


def solution(mesh):
    layered = P(SECTION, None)
    attention = P(SECTION, None, None, TENSOR)
    out = P(SECTION, TENSOR, None)
    experts_in = P(SECTION, EXPERT, None, TENSOR)
    experts_back = P(SECTION, EXPERT, TENSOR, None)
    images = P(SECTION, EXPERT, None, None)
    router = P(SECTION, None, None)
    return jax.shard_map(
        program,
        mesh=mesh,
        in_specs=(
            P(EXPERT, None, None),
            P(EXPERT, None),
            layered,
            layered,
            attention,
            out,
            layered,
            layered,
            router,
            experts_in,
            experts_back,
            images,
            images,
            P(EXPERT, None, None),
        ),
        out_specs=(
            images,
            images,
            layered,
            layered,
            attention,
            out,
            layered,
            layered,
            router,
            experts_in,
            experts_back,
        ),
        check_vma=False,
    )
```

time: 2720 us -> 760 us (0.28)
  waiting for transfers between devices: 1370 us -> 296 us
  blocking collectives: 482 us -> 0 us
  local copies, waits for them, and re-layouts: 397 us -> 28.3 us
  matrix products: 269 us -> 0 us
  Pallas kernels: 0 us -> 196 us
  starting transfers between devices: 39.8 us -> 211 us
  other arithmetic: 125 us -> 21.5 us
    psum x11 -> x0, waiting for transfers between devices: 591 us -> none  [the longest x5 288 us: forward_layer(): lax.psum(jnp.dot(mixed_heads, wout, preferred_element_type=jnp.float32),...]
    all_to_all x15 -> x0, blocking collectives: 397 us -> none  [the longest x5 207 us: forward_layer(): lax.all_to_all(sent_rows, 'expert', split_axis=1, concat_axis=1, tiled=True)]
    reduce_scatter x10 -> x0, waiting for transfers between devices: 385 us -> none  [the longest x5 211 us: forward_layer(): lax.psum_scatter(partial_value, 'tensor', scatter_dimension=2, tiled=True)]
    all_gather x15 -> x0, waiting for transfers between devices: 335 us -> none  [the longest x5 145 us: backward_layer(): grad_arrived = lax.all_gather(arrived_part, 'tensor', axis=2, tiled=True)]
    ppermute x8 -> x186, waiting for transfers between devices: 12.5 us -> 296 us  [the longest x45 198 us: across(): return lax.ppermute(value, TENSOR, [(i, i ^ flip) for i in range(count)])]
    dot_general x120 -> x0, matrix products: 264 us -> none  [the longest x5 27.5 us: backward_layer(): jnp.einsum('erd,efd->erf', grad_arrived, wback, preferred_element_type=jn...]
    ppermute x8 -> x186, starting transfers between devices: 12.7 us -> 211 us  [the longest x56 102 us: hop(): return lax.ppermute(value, (EXPERT, TENSOR), pairs)]
    pallas_call x0 -> x32, Pallas kernels: none -> 196 us  [run(): pl.pallas_call(kernel, out_shape=tuple(shapes), in_specs=in_specs, out_sp...]
  transfers between devices with their start and end apart: 49 -> 186, of which waited for: 43 -> 55; matrix products, arithmetic and copies ran while one was open for 12% -> 5% of each run, Pallas kernels for 0% -> 23%
where the time goes in v1:
time: 760 us; the launch traced here: 755 us
  waiting for transfers between devices  296 us (39%)
  starting transfers between devices  211 us (28%)
  Pallas kernels  196 us (26%)
  local copies, waits for them, and re-layouts  28.3 us (4%)
  other arithmetic  21.5 us (3%)
    ppermute x45, waiting for transfers between devices, across(): return lax.ppermute(value, TENSOR, [(i, i ^ flip) for i in range(count)])  198 us
    pallas_call x32, Pallas kernels, run(): pl.pallas_call(kernel, out_shape=tuple(shapes), in_specs=in_specs, out_sp...  196 us
    ppermute x56, starting transfers between devices, hop(): return lax.ppermute(value, (EXPERT, TENSOR), pairs)  102 us
    ppermute x56, waiting for transfers between devices, hop(): return lax.ppermute(value, (EXPERT, TENSOR), pairs)  64.8 us
    ppermute x45, starting transfers between devices, across(): return lax.ppermute(value, TENSOR, [(i, i ^ flip) for i in range(count)])  54.5 us
    ppermute x10, starting transfers between devices, to_owner(): return lax.ppermute(value, SECTION, [(1 - layer, layer)])  19.6 us
    ppermute x66, starting transfers between devices, swap(): return lax.ppermute(value, SECTION, [(0, 1), (1, 0)])  19.6 us
    unnamed x361, local copies, waits for them, and re-layouts  19.1 us
  transfers between devices with their start and end apart: 186, of which 55 were waited for; matrix products, arithmetic and copies ran while one was open for 5% of the time, Pallas kernels for 23%

profile of v1, /device:TPU:0, one launch (start us, length us, event | category | flops | bytes accessed | tf_op | source)
XLA Modules:
  0.0 754.7 jit_solution(1131005718681294522)
XLA Ops:
  44.0 8.2 %shard_map.222 = (bf16[208,192]{1,0:T(8,128)(2,1)}, bf16[208,192]{1,0:T(8,128)(2,1)}, bf16[208,192]{1,0:T(8,128)(2,1)}, bf16[208,192]{1,0:T(8,128)(2,1)}, bf16[2...) custom-call(s32[4]{0:T(128)} %pad_add_fusion.refs_0_.refs_4_, ...), custom_call_target="tpu_custom_call" | custom-call | flops 1513095168 | bytes 5824560 | tf_op jit(solution)/shard_map/pallas_call | solution.py:110
  54.3 23.2 %collective-permute-done.4.refs_3_ = bf16[208,192]{1,0:T(8,128)(2,1)S(1)} collective-permute-done((bf16[208,192]{1,0:T(8,128)(2,1)}, bf16[208,192]{1,0:T(8,128)(2,1)S(1)}, u32[]{:S(2)}, u32[]{:S(2)}) %collective-permute-start.4) | collective-permute-done | bytes 79904 | tf_op jit(solution)/shard_map/ppermute | solution.py:30
  101.3 9.8 %collective-permute-done.48.refs_25_.refs_8_ = bf16[384,768]{1,0:T(8,128)(2,1)} collective-permute-done((bf16[384,768]{1,0:T(8,128)(2,1)S(1)}, bf16[384,768]{1,0:T(8,128)(2,1)}, u32[]{:S(2)}, u32[]{:S(2)}) %collective-permute-start.48) | collective-permute-done | bytes 589856 | tf_op jit(solution)/shard_map/ppermute | solution.py:30
  127.7 7.6 %collective-permute-done.20.refs_6_ = bf16[64,768]{1,0:T(8,128)(2,1)S(1)} collective-permute-done((bf16[64,768]{1,0:T(8,128)(2,1)S(1)}, bf16[64,768]{1,0:T(8,128)(2,1)S(1)}, u32[]{:S(2)}, u32[]{:S(2)}) %collective-permute-start.20) | collective-permute-done | bytes 98336 | tf_op jit(solution)/shard_map/ppermute | solution.py:45
  135.3 6.4 collective-permute-done.21.refs_7_
  149.7 11.1 %collective-permute-done.25.refs_12_.refs_15_ = bf16[768,768]{1,0:T(8,128)(2,1)} collective-permute-done((bf16[768,768]{1,0:T(8,128)(2,1)}, bf16[768,768]{1,0:T(8,128)(2,1)}, u32[]{:S(2)}, u32[]{:S(2)}) %collective-permute-start.25) | collective-permute-done | bytes 1179680 | tf_op jit(solution)/shard_map/ppermute | solution.py:30
  165.0 11.4 %shard_map.225 = (bf16[512,768]{1,0:T(8,128)(2,1)}, bf16[64,768]{1,0:T(8,128)(2,1)}, bf16[64,768]{1,0:T(8,128)(2,1)}, bf16[64,768]{1,0:T(8,128)(2,1)}, bf16[64,7...) custom-call(s32[4]{0:T(128)} %pad_add_fusion.refs_0_.refs_4_, ...), custom_call_target="tpu_custom_call" | custom-call | flops 4831838208 | bytes 18087952 | tf_op jit(solution)/shard_map/pallas_call | solution.py:110
  180.0 10.1 %collective-permute-done.66.refs_11_.refs_14_ = bf16[768,768]{1,0:T(8,128)(2,1)} collective-permute-done((bf16[768,768]{1,0:T(8,128)(2,1)}, bf16[768,768]{1,0:T(8,128)(2,1)}, u32[]{:S(2)}, u32[]{:S(2)}) %collective-permute-start.66) | collective-permute-done | bytes 1179680 | tf_op jit(solution)/shard_map/ppermute | solution.py:30
  192.6 22.2 %collective-permute-done.67.refs_12_.refs_15_ = bf16[768,768]{1,0:T(8,128)(2,1)} collective-permute-done((bf16[768,768]{1,0:T(8,128)(2,1)}, bf16[768,768]{1,0:T(8,128)(2,1)}, u32[]{:S(2)}, u32[]{:S(2)}) %collective-permute-start.67) | collective-permute-done | bytes 1179680 | tf_op jit(solution)/shard_map/ppermute | solution.py:30
  241.4 11.1 %shard_map.226 = (bf16[208,768]{1,0:T(8,128)(2,1)}, bf16[2,208,768]{2,1,0:T(8,128)(2,1)}, f32[208,768]{1,0:T(8,128)}, bf16[208,768]{1,0:T(8,128)(2,1)}, f32[208,...) custom-call(s32[4]{0:T(128)} %pad_add_fusion.refs_0_.refs_4_, ...), custom_call_target="tpu_custom_call" | custom-call | flops 1513095168 | bytes 10494992 | tf_op jit(solution)/shard_map/pallas_call | solution.py:110
  281.7 5.6 collective-permute-done.61.refs_6_
  287.3 5.7 collective-permute-start.98
  293.6 11.4 %shard_map.228 = (bf16[512,768]{1,0:T(8,128)(2,1)}, bf16[64,768]{1,0:T(8,128)(2,1)}, bf16[64,768]{1,0:T(8,128)(2,1)}, bf16[64,768]{1,0:T(8,128)(2,1)}, bf16[64,7...) custom-call(s32[4]{0:T(128)} %pad_add_fusion.refs_0_.refs_4_, ...), custom_call_target="tpu_custom_call" | custom-call | flops 4831838208 | bytes 18087952 | tf_op jit(solution)/shard_map/pallas_call | solution.py:110
  305.9 13.5 %shard_map.234 = (bf16[512,768]{1,0:T(8,128)(2,1)}, bf16[64,768]{1,0:T(8,128)(2,1)}, bf16[64,768]{1,0:T(8,128)(2,1)}, bf16[64,768]{1,0:T(8,128)(2,1)}, bf16[64,7...) custom-call(s32[4]{0:T(128)} %pad_add_fusion.refs_0_.refs_4_, ...), custom_call_target="tpu_custom_call" | custom-call | flops 4831838208 | bytes 25952272 | tf_op jit(solution)/shard_map/pallas_call | solution.py:110
  320.4 8.9 %collective-permute-start.101 = (bf16[64,768]{1,0:T(8,128)(2,1)}, bf16[64,768]{1,0:T(8,128)(2,1)S(1)}, u32[]{:S(2)}, u32[]{:S(2)}) collective-permute-start(bf16[64,768]{1,0:T(8,128)(2,1)} %get-tuple-element.226), channel_id=1, source_target_pairs={{0,4},{1,5},{2,6},{3,7},{4,0},{5,1},{6,2},{7,3},{8,12},{9,13},{10,... | collective-permute-start | bytes 294920 | tf_op jit(solution)/shard_map/ppermute | solution.py:45
  376.7 11.9 %shard_map.236 = (bf16[208,768]{1,0:T(8,128)(2,1)}, bf16[240,1536]{1,0:T(8,128)(2,1)}, bf16[208,768]{1,0:T(8,128)(2,1)}, bf16[208,768]{1,0:T(8,128)(2,1)}, bf16[...) custom-call(s32[4]{0:T(128)} %pad_add_fusion.refs_0_.refs_4_, bf16[208,768]{1,0:T(8,128)(2,1)} %get-tuple-element.189.refs_0_.refs_2_.refs_1_, ...), custom_call_target="tpu_custom_call" | custom-call | flops 3026190336 | bytes 9777168 | tf_op jit(solution)/shard_map/pallas_call | solution.py:110
  424.6 13.3 %shard_map.238 = (bf16[512,768]{1,0:T(8,128)(2,1)}, bf16[64,768]{1,0:T(8,128)(2,1)}, bf16[64,768]{1,0:T(8,128)(2,1)}, bf16[64,768]{1,0:T(8,128)(2,1)}, bf16[64,7...) custom-call(s32[4]{0:T(128)} %pad_add_fusion.refs_0_.refs_4_, ...), custom_call_target="tpu_custom_call" | custom-call | flops 4831838208 | bytes 25952272 | tf_op jit(solution)/shard_map/pallas_call | solution.py:110
  442.0 6.7 collective-permute-done.88.refs_2_.refs_8_
  459.5 6.5 collective-permute-done.127.refs_6_
  486.0 13.3 %shard_map.240 = (bf16[208,768]{1,0:T(8,128)(2,1)}, bf16[240,576]{1,0:T(8,128)(2,1)}, bf16[240,576]{1,0:T(8,128)(2,1)}, bf16[240,576]{1,0:T(8,128)(2,1)}, bf16[240,576]{1,0:T(8,128)(2,1)}) custom-call(s32[4]{0:T(128)} %pad_add_fusion.refs_0_.refs_4_, bf16[208,768]{1,0:T(8,128)(2,1)} %get-tuple-element.163.refs_1_, ...), custom_call_target="tpu_custom_call" | custom-call | flops 3026190336 | bytes 7483408 | tf_op jit(solution)/shard_map/pallas_call | solution.py:110
  506.3 7.5 collective-permute-done.154.refs_6_
  516.1 10.3 %collective-permute-done.156.refs_8_ = bf16[240,576]{1,0:T(8,128)(2,1)S(1)} collective-permute-done((bf16[240,576]{1,0:T(8,128)(2,1)}, bf16[240,576]{1,0:T(8,128)(2,1)S(1)}, u32[]{:S(2)}, u32[]{:S(2)}) %collective-permute-start.156) | collective-permute-done | bytes 276512 | tf_op jit(solution)/shard_map/ppermute | solution.py:30
  530.4 21.1 %collective-permute-done.159.refs_12_ = bf16[224,768]{1,0:T(8,128)(2,1)} collective-permute-done((bf16[224,768]{1,0:T(8,128)(2,1)}, bf16[224,768]{1,0:T(8,128)(2,1)}, u32[]{:S(2)}, u32[]{:S(2)}) %collective-permute-start.159) | collective-permute-done | bytes 344096 | tf_op jit(solution)/shard_map/ppermute | solution.py:30
  563.4 6.2 shard_map.245
  571.3 10.9 %shard_map.251 = (bf16[768,768]{1,0:T(8,128)(2,1)}, bf16[768,768]{1,0:T(8,128)(2,1)}, bf16[768,768]{1,0:T(8,128)(2,1)}, bf16[768,768]{1,0:T(8,128)(2,1)}) custom-call(s32[4]{0:T(128)} %pad_add_fusion.refs_0_.refs_4_, bf16[512,768]{1,0:T(8,128)(2,1)} %get-tuple-element.221.refs_9_.refs_1_, bf16[512,768]{1,0:T(8,128)(2,1)} %get-tuple-element.301.refs_2_, ...), custom_call_target="tpu_custom_call" | custom-call | flops 4831838208 | bytes 16515088 | tf_op jit(solution)/shard_map/pallas_call | solution.py:110
  585.9 10.9 %shard_map.250 = (bf16[768,768]{1,0:T(8,128)(2,1)}, bf16[768,768]{1,0:T(8,128)(2,1)}, bf16[768,768]{1,0:T(8,128)(2,1)}, bf16[768,768]{1,0:T(8,128)(2,1)}) custom-call(s32[4]{0:T(128)} %pad_add_fusion.refs_0_.refs_4_, bf16[512,768]{1,0:T(8,128)(2,1)} %get-tuple-element.251.refs_9_.refs_1_, bf16[512,768]{1,0:T(8,128)(2,1)} %get-tuple-element.293.refs_2_, ...), custom_call_target="tpu_custom_call" | custom-call | flops 4831838208 | bytes 16515088 | tf_op jit(solution)/shard_map/pallas_call | solution.py:110
  619.6 6.5 collective-permute-done.180
  628.0 23.3 %collective-permute-done.175 = bf16[768,768]{1,0:T(8,128)(2,1)} collective-permute-done((bf16[768,768]{1,0:T(8,128)(2,1)}, bf16[768,768]{1,0:T(8,128)(2,1)}, u32[]{:S(2)}, u32[]{:S(2)}) %collective-permute-start.175) | collective-permute-done | bytes 1179680 | tf_op jit(solution)/shard_map/ppermute | solution.py:30
  667.9 8.8 %collective-permute-done.179 = bf16[768,768]{1,0:T(8,128)(2,1)} collective-permute-done((bf16[768,768]{1,0:T(8,128)(2,1)}, bf16[768,768]{1,0:T(8,128)(2,1)}, u32[]{:S(2)}, u32[]{:S(2)}) %collective-permute-start.179) | collective-permute-done | bytes 1179680 | tf_op jit(solution)/shard_map/ppermute | solution.py:30
  678.7 6.3 collective-permute-done.168.refs_2_
  685.7 15.7 %collective-permute-done.174 = bf16[768,768]{1,0:T(8,128)(2,1)} collective-permute-done((bf16[768,768]{1,0:T(8,128)(2,1)}, bf16[768,768]{1,0:T(8,128)(2,1)}, u32[]{:S(2)}, u32[]{:S(2)}) %collective-permute-start.174) | collective-permute-done | bytes 1179680 | tf_op jit(solution)/shard_map/ppermute | solution.py:30
  747.7 6.8 shard_map.252
  (754 shorter events, 400.0 us)
Async XLA Ops:
  13.6 87.7 %collective-permute-start.64 = (bf16[2,768,768]{2,1,0:T(8,128)(2,1)}, bf16[2,768,768]{2,1,0:T(8,128)(2,1)}, u32[]{:S(2)}, u32[]{:S(2)}) collective-permute-start(bf16[2,768,768]{2,1,0:T(8,128)(2,1)} %bitcast.46), channel_id=1, source_target_pairs={{16,0},{17,1},{18,2},{19,3},{20,4},{21,5},{22,6},{23,7},{24,8},{25... | collective-permute-start | bytes 7077896 | tf_op jit(solution)/shard_map/ppermute | solution.py:53
  32.6 65.1 %collective-permute-start.23 = (bf16[768,768]{1,0:T(8,128)(2,1)}, bf16[768,768]{1,0:T(8,128)(2,1)}, u32[]{:S(2)}, u32[]{:S(2)}) collective-permute-start(bf16[768,768]{1,0:T(8,128)(2,1)} %get-tuple-element.324), channel_id=1, source_target_pairs={{0,1},{1,0},{2,3},{3,2},{4,5},{5,4},{6,7},{7,6},{8,9},{9,8},{10,11... | collective-permute-start | bytes 3538952 | tf_op jit(solution)/shard_map/ppermute | solution.py:30
  39.9 54.3 %collective-permute-start.46 = (bf16[384,768]{1,0:T(8,128)(2,1)S(1)}, bf16[384,768]{1,0:T(8,128)(2,1)S(1)}, u32[]{:S(2)}, u32[]{:S(2)}) collective-permute-start(bf16[384,768]{1,0:T(8,128)(2,1)S(1)} %maximum_select_fusion.refs_22_.refs_5_), channel_id=1, source_target_pairs={{0,1},{1,0},{2,3},{3,2},{4,5},{5,4},{6,7},{7,6},{8,9},{9,8},{10,11... | collective-permute-start | bytes 1769480 | tf_op jit(solution)/shard_map/ppermute | solution.py:30
  43.4 51.4 %collective-permute-start.47 = (bf16[384,768]{1,0:T(8,128)(2,1)S(1)}, bf16[384,768]{1,0:T(8,128)(2,1)}, u32[]{:S(2)}, u32[]{:S(2)}) collective-permute-start(bf16[384,768]{1,0:T(8,128)(2,1)S(1)} %maximum_select_fusion.refs_22_.refs_5_), channel_id=1, source_target_pairs={{0,2},{1,3},{2,0},{3,1},{4,6},{5,7},{6,4},{7,5},{8,10},{9,11},{10,... | collective-permute-start | bytes 1769480 | tf_op jit(solution)/shard_map/ppermute | solution.py:30
  96.3 52.7 %collective-permute-start.24 = (bf16[768,768]{1,0:T(8,128)(2,1)}, bf16[768,768]{1,0:T(8,128)(2,1)}, u32[]{:S(2)}, u32[]{:S(2)}) collective-permute-start(bf16[768,768]{1,0:T(8,128)(2,1)} %get-tuple-element.325.refs_9_.refs_12_), channel_id=1, source_target_pairs={{0,2},{1,3},{2,0},{3,1},{4,6},{5,7},{6,4},{7,5},{8,10},{9,11},{10,... | collective-permute-start | bytes 3538952 | tf_op jit(solution)/shard_map/ppermute | solution.py:30
  97.7 63.1 %collective-permute-start.25 = (bf16[768,768]{1,0:T(8,128)(2,1)}, bf16[768,768]{1,0:T(8,128)(2,1)}, u32[]{:S(2)}, u32[]{:S(2)}) collective-permute-start(bf16[768,768]{1,0:T(8,128)(2,1)} %collective-permute-done.23.refs_10_.refs_13_), channel_id=1, source_target_pairs={{0,2},{1,3},{2,0},{3,1},{4,6},{5,7},{6,4},{7,5},{8,10},{9,11},{10,... | collective-permute-start | bytes 3538952 | tf_op jit(solution)/shard_map/ppermute | solution.py:30
  101.3 59.5 %collective-permute-start.26 = (bf16[768,768]{1,0:T(8,128)(2,1)}, bf16[768,768]{1,0:T(8,128)(2,1)S(1)}, u32[]{:S(2)}, u32[]{:S(2)}) collective-permute-start(bf16[768,768]{1,0:T(8,128)(2,1)} %get-tuple-element.325.refs_9_.refs_12_), channel_id=1, source_target_pairs={{0,16},{16,0},{1,17},{17,1},{2,18},{18,2},{3,19},{19,3},{4,20},{20... | collective-permute-start | bytes 3538952 | tf_op jit(solution)/shard_map/ppermute | solution.py:25
  116.5 45.9 %collective-permute-start.65 = (bf16[768,768]{1,0:T(8,128)(2,1)S(1)}, bf16[768,768]{1,0:T(8,128)(2,1)}, u32[]{:S(2)}, u32[]{:S(2)}) collective-permute-start(bf16[768,768]{1,0:T(8,128)(2,1)S(1)} %get-tuple-element.322), channel_id=1, source_target_pairs={{0,1},{1,0},{2,3},{3,2},{4,5},{5,4},{6,7},{7,6},{8,9},{9,8},{10,11... | collective-permute-start | bytes 3538952 | tf_op jit(solution)/shard_map/ppermute | solution.py:30
  162.4 52.4 %collective-permute-start.67 = (bf16[768,768]{1,0:T(8,128)(2,1)}, bf16[768,768]{1,0:T(8,128)(2,1)}, u32[]{:S(2)}, u32[]{:S(2)}) collective-permute-start(bf16[768,768]{1,0:T(8,128)(2,1)} %collective-permute-done.65.refs_10_.refs_13_), channel_id=1, source_target_pairs={{0,2},{1,3},{2,0},{3,1},{4,6},{5,7},{6,4},{7,5},{8,10},{9,11},{10,... | collective-permute-start | bytes 3538952 | tf_op jit(solution)/shard_map/ppermute | solution.py:30
  176.4 40.9 %collective-permute-start.30 = (bf16[64,768]{1,0:T(8,128)(2,1)}, bf16[64,768]{1,0:T(8,128)(2,1)S(1)}, u32[]{:S(2)}, u32[]{:S(2)}) collective-permute-start(bf16[64,768]{1,0:T(8,128)(2,1)} %get-tuple-element.180), channel_id=1, source_target_pairs={{0,1},{1,0},{2,3},{3,2},{4,5},{5,4},{6,7},{7,6},{8,9},{9,8},{10,11... | collective-permute-start | bytes 294920 | tf_op jit(solution)/shard_map/ppermute | solution.py:45
  176.8 41.9 %collective-permute-start.31 = (bf16[64,768]{1,0:T(8,128)(2,1)}, bf16[64,768]{1,0:T(8,128)(2,1)S(1)}, u32[]{:S(2)}, u32[]{:S(2)}) collective-permute-start(bf16[64,768]{1,0:T(8,128)(2,1)} %get-tuple-element.181), channel_id=1, source_target_pairs={{0,4},{1,5},{2,6},{3,7},{4,0},{5,1},{6,2},{7,3},{8,12},{9,13},{10,... | collective-permute-start | bytes 294920 | tf_op jit(solution)/shard_map/ppermute | solution.py:45
  178.6 43.5 %collective-permute-start.32 = (bf16[64,768]{1,0:T(8,128)(2,1)}, bf16[64,768]{1,0:T(8,128)(2,1)S(1)}, u32[]{:S(2)}, u32[]{:S(2)}) collective-permute-start(bf16[64,768]{1,0:T(8,128)(2,1)} %get-tuple-element.182), channel_id=1, source_target_pairs={{0,5},{1,4},{2,7},{3,6},{4,1},{5,0},{6,3},{7,2},{8,13},{9,12},{10,... | collective-permute-start | bytes 294920 | tf_op jit(solution)/shard_map/ppermute | solution.py:45
  228.2 35.3 %collective-permute-start.68 = (bf16[768,768]{1,0:T(8,128)(2,1)}, bf16[768,768]{1,0:T(8,128)(2,1)}, u32[]{:S(2)}, u32[]{:S(2)}) collective-permute-start(bf16[768,768]{1,0:T(8,128)(2,1)} %get-tuple-element.323.refs_9_.refs_12_), channel_id=1, source_target_pairs={{0,16},{16,0},{1,17},{17,1},{2,18},{18,2},{3,19},{19,3},{4,20},{20... | collective-permute-start | bytes 3538952 | tf_op jit(solution)/shard_map/ppermute | solution.py:25
  228.7 37.1 %collective-permute-start.69 = (bf16[768,768]{1,0:T(8,128)(2,1)}, bf16[768,768]{1,0:T(8,128)(2,1)}, u32[]{:S(2)}, u32[]{:S(2)}) collective-permute-start(bf16[768,768]{1,0:T(8,128)(2,1)} %collective-permute-done.65.refs_10_.refs_13_), channel_id=1, source_target_pairs={{0,16},{16,0},{1,17},{17,1},{2,18},{18,2},{3,19},{19,3},{4,20},{20... | collective-permute-start | bytes 3538952 | tf_op jit(solution)/shard_map/ppermute | solution.py:25
  228.8 38.1 %collective-permute-start.70 = (bf16[768,768]{1,0:T(8,128)(2,1)}, bf16[768,768]{1,0:T(8,128)(2,1)}, u32[]{:S(2)}, u32[]{:S(2)}) collective-permute-start(bf16[768,768]{1,0:T(8,128)(2,1)} %collective-permute-done.66.refs_11_.refs_14_), channel_id=1, source_target_pairs={{0,16},{16,0},{1,17},{17,1},{2,18},{18,2},{3,19},{19,3},{4,20},{20... | collective-permute-start | bytes 3538952 | tf_op jit(solution)/shard_map/ppermute | solution.py:25
  229.4 37.5 %collective-permute-start.71 = (bf16[768,768]{1,0:T(8,128)(2,1)}, bf16[768,768]{1,0:T(8,128)(2,1)}, u32[]{:S(2)}, u32[]{:S(2)}) collective-permute-start(bf16[768,768]{1,0:T(8,128)(2,1)} %collective-permute-done.67.refs_12_.refs_15_), channel_id=1, source_target_pairs={{0,16},{16,0},{1,17},{17,1},{2,18},{18,2},{3,19},{19,3},{4,20},{20... | collective-permute-start | bytes 3538952 | tf_op jit(solution)/shard_map/ppermute | solution.py:25
  418.1 152.3 %collective-permute-start.178 = (bf16[4,512,768]{2,1,0:T(8,128)(2,1)}, bf16[4,512,768]{2,1,0:T(8,128)(2,1)}, u32[]{:S(2)}, u32[]{:S(2)}) collective-permute-start(bf16[4,512,768]{2,1,0:T(8,128)(2,1)} %get-tuple-element.304), channel_id=1, source_target_pairs={{0,16},{16,0},{1,17},{17,1},{2,18},{18,2},{3,19},{19,3},{4,20},{20... | collective-permute-start | bytes 9437192 | tf_op jit(solution)/shard_map/ppermute | solution.py:25
  438.0 147.9 %collective-permute-start.173 = (bf16[4,512,768]{2,1,0:T(8,128)(2,1)}, bf16[4,512,768]{2,1,0:T(8,128)(2,1)}, u32[]{:S(2)}, u32[]{:S(2)}) collective-permute-start(bf16[4,512,768]{2,1,0:T(8,128)(2,1)} %get-tuple-element.296), channel_id=1, source_target_pairs={{0,16},{16,0},{1,17},{17,1},{2,18},{18,2},{3,19},{19,3},{4,20},{20... | collective-permute-start | bytes 9437192 | tf_op jit(solution)/shard_map/ppermute | solution.py:25
  526.5 35.4 %collective-permute-start.151 = (bf16[240,1536]{1,0:T(8,128)(2,1)S(1)}, bf16[240,1536]{1,0:T(8,128)(2,1)S(1)}, u32[]{:S(2)}, u32[]{:S(2)}) collective-permute-start(bf16[240,1536]{1,0:T(8,128)(2,1)S(1)} %collective-permute-done.150.refs_2_.refs_8_.refs_11_), channel_id=1, source_target_pairs={{0,1},{1,0},{2,3},{3,2},{4,5},{5,4},{6,7},{7,6},{8,9},{9,8},{10,11... | collective-permute-start | bytes 2211848 | tf_op jit(solution)/shard_map/ppermute | solution.py:30
  527.4 42.2 %collective-permute-start.177 = (bf16[512,768]{1,0:T(8,128)(2,1)}, bf16[512,768]{1,0:T(8,128)(2,1)}, u32[]{:S(2)}, u32[]{:S(2)}) collective-permute-start(bf16[512,768]{1,0:T(8,128)(2,1)} %get-tuple-element.303), channel_id=1, source_target_pairs={{0,16},{16,0},{1,17},{17,1},{2,18},{18,2},{3,19},{19,3},{4,20},{20... | collective-permute-start | bytes 2359304 | tf_op jit(solution)/shard_map/ppermute | solution.py:25
  561.8 49.7 %collective-permute-start.90 = (bf16[4,208,768]{2,1,0:T(8,128)(2,1)}, bf16[4,208,768]{2,1,0:T(8,128)(2,1)S(1)}, u32[]{:S(2)}, u32[]{:S(2)}) collective-permute-start(bf16[4,208,768]{2,1,0:T(8,128)(2,1)} %shard_map.230), channel_id=1, source_target_pairs={{16,0},{17,1},{18,2},{19,3},{20,4},{21,5},{22,6},{23,7},{24,8},{25... | collective-permute-start | bytes 3833864 | tf_op jit(solution)/shard_map/ppermute | solution.py:53
  598.1 53.3 %collective-permute-start.175 = (bf16[768,768]{1,0:T(8,128)(2,1)}, bf16[768,768]{1,0:T(8,128)(2,1)}, u32[]{:S(2)}, u32[]{:S(2)}) collective-permute-start(bf16[768,768]{1,0:T(8,128)(2,1)} %get-tuple-element.300), channel_id=1, source_target_pairs={{0,2},{1,3},{2,0},{3,1},{4,6},{5,7},{6,4},{7,5},{8,10},{9,11},{10,... | collective-permute-start | bytes 3538952 | tf_op jit(solution)/shard_map/ppermute | solution.py:30
  611.5 51.7 %collective-permute-start.152 = (bf16[4,208,768]{2,1,0:T(8,128)(2,1)}, bf16[4,208,768]{2,1,0:T(8,128)(2,1)S(1)}, u32[]{:S(2)}, u32[]{:S(2)}) collective-permute-start(bf16[4,208,768]{2,1,0:T(8,128)(2,1)} %shard_map.241), channel_id=1, source_target_pairs={{16,0},{17,1},{18,2},{19,3},{20,4},{21,5},{22,6},{23,7},{24,8},{25... | collective-permute-start | bytes 3833864 | tf_op jit(solution)/shard_map/ppermute | solution.py:53
  612.8 63.8 %collective-permute-start.179 = (bf16[768,768]{1,0:T(8,128)(2,1)}, bf16[768,768]{1,0:T(8,128)(2,1)}, u32[]{:S(2)}, u32[]{:S(2)}) collective-permute-start(bf16[768,768]{1,0:T(8,128)(2,1)} %get-tuple-element.306), channel_id=1, source_target_pairs={{0,2},{1,3},{2,0},{3,1},{4,6},{5,7},{6,4},{7,5},{8,10},{9,11},{10,... | collective-permute-start | bytes 3538952 | tf_op jit(solution)/shard_map/ppermute | solution.py:30
  618.8 39.4 %collective-permute-start.166 = (bf16[2,128,768]{2,1,0:T(8,128)(2,1)}, bf16[2,128,768]{2,1,0:T(8,128)(2,1)S(1)}, u32[]{:S(2)}, u32[]{:S(2)}) collective-permute-start(bf16[2,128,768]{2,1,0:T(8,128)(2,1)} %get-tuple-element.284), channel_id=1, source_target_pairs={{0,8},{4,12},{8,0},{12,4},{1,9},{5,13},{9,1},{13,5},{2,10},{6,14},... | collective-permute-start | bytes 1179656 | tf_op jit(solution)/shard_map/ppermute | solution.py:35
  651.3 50.1 %collective-permute-start.174 = (bf16[768,768]{1,0:T(8,128)(2,1)}, bf16[768,768]{1,0:T(8,128)(2,1)}, u32[]{:S(2)}, u32[]{:S(2)}) collective-permute-start(bf16[768,768]{1,0:T(8,128)(2,1)} %get-tuple-element.298), channel_id=1, source_target_pairs={{0,2},{1,3},{2,0},{3,1},{4,6},{5,7},{6,4},{7,5},{8,10},{9,11},{10,... | collective-permute-start | bytes 3538952 | tf_op jit(solution)/shard_map/ppermute | solution.py:30
  658.2 55.0 %collective-permute-start.181 = (bf16[768,768]{1,0:T(8,128)(2,1)}, bf16[768,768]{1,0:T(8,128)(2,1)}, u32[]{:S(2)}, u32[]{:S(2)}) collective-permute-start(bf16[768,768]{1,0:T(8,128)(2,1)} %add_convert_fusion), channel_id=1, source_target_pairs={{0,1},{1,0},{2,3},{3,2},{4,5},{5,4},{6,7},{7,6},{8,9},{9,8},{10,11... | collective-permute-start | bytes 3538952 | tf_op jit(solution)/shard_map/ppermute | solution.py:30
  659.4 58.9 %collective-permute-start.176 = (bf16[768,768]{1,0:T(8,128)(2,1)}, bf16[768,768]{1,0:T(8,128)(2,1)}, u32[]{:S(2)}, u32[]{:S(2)}) collective-permute-start(bf16[768,768]{1,0:T(8,128)(2,1)} %add_convert_fusion.2), channel_id=1, source_target_pairs={{0,1},{1,0},{2,3},{3,2},{4,5},{5,4},{6,7},{7,6},{8,9},{9,8},{10,11... | collective-permute-start | bytes 3538952 | tf_op jit(solution)/shard_map/ppermute | solution.py:30
  663.2 59.0 %collective-permute-start.153 = (bf16[4,208,768]{2,1,0:T(8,128)(2,1)}, bf16[4,208,768]{2,1,0:T(8,128)(2,1)}, u32[]{:S(2)}, u32[]{:S(2)}) collective-permute-start(bf16[4,208,768]{2,1,0:T(8,128)(2,1)} %shard_map.242), channel_id=1, source_target_pairs={{0,16},{1,17},{2,18},{3,19},{4,20},{5,21},{6,22},{7,23},{8,24},{9,... | collective-permute-start | bytes 3833864 | tf_op jit(solution)/shard_map/ppermute | solution.py:53
  705.0 41.7 %collective-permute-start.184 = (bf16[768,768]{1,0:T(8,128)(2,1)S(1)}, bf16[768,768]{1,0:T(8,128)(2,1)S(1)}, u32[]{:S(2)}, u32[]{:S(2)}) collective-permute-start(bf16[768,768]{1,0:T(8,128)(2,1)S(1)} %add_convert_fusion.1.refs_3_), channel_id=1, source_target_pairs={{0,16},{1,17},{2,18},{3,19},{4,20},{5,21},{6,22},{7,23},{8,24},{9,... | collective-permute-start | bytes 3538952 | tf_op jit(solution)/shard_map/ppermute | solution.py:53
  711.9 34.8 %collective-permute-start.182 = (bf16[768,768]{1,0:T(8,128)(2,1)S(1)}, bf16[768,768]{1,0:T(8,128)(2,1)}, u32[]{:S(2)}, u32[]{:S(2)}) collective-permute-start(bf16[768,768]{1,0:T(8,128)(2,1)S(1)} %add_convert_fusion.3.refs_1_), channel_id=1, source_target_pairs={{16,0},{17,1},{18,2},{19,3},{20,4},{21,5},{22,6},{23,7},{24,8},{25... | collective-permute-start | bytes 3538952 | tf_op jit(solution)/shard_map/ppermute | solution.py:53
  713.2 33.5 %collective-permute-start.185 = (bf16[768,768]{1,0:T(8,128)(2,1)}, bf16[768,768]{1,0:T(8,128)(2,1)}, u32[]{:S(2)}, u32[]{:S(2)}) collective-permute-start(bf16[768,768]{1,0:T(8,128)(2,1)} %collective-permute-done.181.refs_4_), channel_id=1, source_target_pairs={{0,16},{1,17},{2,18},{3,19},{4,20},{5,21},{6,22},{7,23},{8,24},{9,... | collective-permute-start | bytes 3538952 | tf_op jit(solution)/shard_map/ppermute | solution.py:53
  (333 other events, 4746.3 us)

commit v2 on v1

--- a/solution.py
+++ b/solution.py
@@ -43,14 +43,6 @@
         for t in range(count)
     ]
     return lax.ppermute(value, (EXPERT, TENSOR), pairs)
-
-
-def to_sibling(value, layer):
-    return lax.ppermute(value, SECTION, [(layer, 1 - layer)])
-
-
-def to_owner(value, layer):
-    return lax.ppermute(value, SECTION, [(1 - layer, layer)])
 
 
 def V(value):
@@ -684,12 +676,11 @@
             ).start()
         arrived(ns.fixed.at[0:size], ns.fixed_sem.at[0])
         arrived(ns.fixed.at[size:], ns.fixed_sem.at[1])
-        ns.turned[...] = ns.fixed[...].T
 
         def chunk(d, carry):
             arrived(ns.moving.at[d, 0:size], ns.sem.at[0, d])
             arrived(ns.moving.at[d, size:], ns.sem.at[1, d])
-            ns.out_s[d] = dot(ns.turned[...], ns.moving[d]).astype(LOW)
+            ns.out_s[d] = dot_tn(ns.fixed[...], ns.moving[d]).astype(LOW)
             for k in range(cfg.tensor):
 
                 @pl.when(d == k)
@@ -715,7 +706,6 @@
     outs = dict(out=O(shape, LOW, cfg.tensor, space=pl.ANY))
     scratch = dict(
         fixed=pltpu.VMEM((2 * size, cfg.width), LOW),
-        turned=pltpu.VMEM((cfg.width, 2 * size), LOW),
         moving=pltpu.VMEM((cfg.tensor, 2 * size, cfg.hidden), LOW),
         out_s=pltpu.VMEM((cfg.tensor,) + shape, LOW),
         fixed_sem=pltpu.SemaphoreType.DMA((2,)),
@@ -913,15 +903,15 @@
         ns.keep[0:rest, :] = jnp.where(first, low, high)
         ns.send[0:rest, :] = jnp.where(first, high, low).astype(LOW)
         upper, lower = pair_sum(upper), pair_sum(lower)
-        ns.keep[rest : rest + small, :] = upper
-        ns.keep[rest + small :, :] = lower
-        ns.send[rest : rest + small, :] = upper.astype(LOW)
-        ns.send[rest + small :, :] = lower.astype(LOW)
+        place = cfg.experts + 2
+        ns.keep[rest:, :] = upper
+        ns.keep[rest + place : rest + place + 2, :] = lower[0:2, :]
+        ns.send[rest:, :] = ns.keep[rest:, :].astype(LOW)
 
     ins = dict(info=S(cfg.info), rows=V(rows), sent=V(sent), datt=V(datt), pack=V(pack))
     if not joined:
         ins.update(mixed=V(mixed))
-    shape = (2 * cols + small + 16, width)
+    shape = (2 * cols + small, width)
     outs = dict(keep=O(shape, F32), send=O(shape, LOW))
     every = cfg.tensor * padded
     scratch = dict(
@@ -947,7 +937,7 @@
                 ns.pieces[z][layer, part:, :] = ns.total[rest:, :].astype(LOW)
 
     ins = dict(info=S(cfg.info), keep=V(keeps), received=V(received))
-    outs = dict(pieces=O((2, part + cfg.small + 16, cfg.width), LOW, cfg.owners))
+    outs = dict(pieces=O((2, part + cfg.small, cfg.width), LOW, cfg.owners))
     scratch = dict(total=pltpu.VMEM(keeps[0].shape, F32))
     return run(body, ins, outs, scratch).pieces
 
@@ -961,7 +951,7 @@
         ns.small[...] = total[:, part:, :]
 
     outs = dict(
-        total=O((2, part, cfg.width), LOW), small=O((2, cfg.small + 16, cfg.width), F32)
+        total=O((2, part, cfg.width), LOW), small=O((2, cfg.small, cfg.width), F32)
     )
     return run(body, dict(pieces=V(pieces)), outs)
 
@@ -1045,24 +1035,14 @@
     return run(body, ins, outs, scratch)
 
 
-def stack_images(values, place):
-    low, high, left, right = place
-
-    def body(ns):
-        for d, value in enumerate(ns.values):
-            ns.out[d] = value[low:high, left:right]
-
-    outs = dict(out=O((len(values), high - low, right - left), LOW))
-    return run(body, dict(values=V(values)), outs).out
-
-
 def place_images(cfg, mine, theirs, lefts, dtype):
     def body(ns):
         def place_layer(own, other, left):
             for d in range(cfg.tensor):
                 image = own[d][0 : cfg.seq, left : left + cfg.width]
                 ns.images[0, image_of(ns, d, 0)] = image.astype(dtype)
-                ns.images[0, image_of(ns, d, 1)] = other[d, 0 : cfg.seq, :].astype(dtype)
+                image = other[d][0 : cfg.seq, left : left + cfg.width]
+                ns.images[0, image_of(ns, d, 1)] = image.astype(dtype)
 
         pl.when(ns.info[0] == 0)(lambda: place_layer(ns.mine0, ns.theirs0, lefts[0]))
         pl.when(ns.info[0] == 1)(lambda: place_layer(ns.mine1, ns.theirs1, lefts[1]))
@@ -1156,7 +1136,7 @@
     experts = local * owners
     capacity = (TOPK * IMG_MB * seq * 5 // (4 * experts) + 7) // 8 * 8
     padded = (seq + 15) // 16 * 16
-    small = (experts + 2 + 15) // 16 * 16
+    small = (experts + 4 + 15) // 16 * 16
     cfg = SimpleNamespace(
         tensor=count,
         owners=owners,
@@ -1181,7 +1161,7 @@
     wq = w_qkv[0].transpose(0, 2, 1).reshape(3 * cfg.cols, width)
     wo = w_out[0]
     wq_half, wo_half = 3 * cfg.cols // 2, cfg.cols // 2
-    sibling_wq = to_sibling(wq, 0)
+    sibling_wq = swap(wq)
     pack = jnp.concatenate([gain_attn, shift_attn, gain_moe, shift_moe, w_router[0].T], axis=0)
     other_pack = swap(pack)
     packs = [
@@ -1200,9 +1180,9 @@
         return lax.dynamic_index_in_dim(values, index, 0, keepdims=False)
 
     weights = [Weights(), Weights()]
-    sibling_wo = to_sibling(wo[wo_half:], 0)
-    sibling_we = to_sibling(w_back[0], 0)
-    wo_own = jnp.where(first_core, wo[:wo_half], sibling_wo)
+    sibling_wo = swap(wo)
+    sibling_we = swap(w_back[0])
+    wo_own = jnp.where(first_core, wo[:wo_half], sibling_wo[wo_half:])
     weights[0].wo_d = gather_images(wo_own)
     weights[0].wo_f = swaps(weights[0].wo_d)
 
@@ -1215,12 +1195,14 @@
     first_pair = pair(w_in[0], sibling_we)
     weights[0].we_d = relay(*first_pair)
     weights[0].we_f = forward_chunks(weights[0].we_d)
-    joined = [jnp.concatenate([wq[:wq_half], wo[:wo_half]], axis=0)]
-    joined.append(jnp.concatenate([wq[wq_half:], wo[wo_half:]], axis=0))
-    joined = jnp.where(first_core, to_owner(joined[0], 0), joined[1])
+    joined = jnp.where(
+        first_core,
+        jnp.concatenate([sibling_wq[:wq_half], sibling_wo[:wo_half]], axis=0),
+        jnp.concatenate([wq[wq_half:], wo[wo_half:]], axis=0),
+    )
     weights[1].wq_d = relay(joined, joined)
     weights[1].wq_f = swaps(weights[1].wq_d)
-    sibling_we = to_owner(w_in[0], 0)
+    sibling_we = swap(w_in[0])
     weights[1].we_d = relay(*pair(sibling_we, w_back[0]))
     weights[1].we_f = forward_chunks(weights[1].we_d)
     wq0_own = jnp.where(first_core, wq[:wq_half], sibling_wq[wq_half:])
@@ -1287,7 +1269,7 @@
         own = add(zero, two)
         expert_grads[layer] = (
             [own, one],
-            [to_owner(own, layer), to_owner(one, layer)],
+            [swap(own), swap(one)],
         )
         upper = back_to_attention(
             cfg,
@@ -1317,17 +1299,11 @@
     piece = sum_pieces(cfg, split)
     pieces = [piece.total] + [along(piece.total, z) for z in range(1, owners)]
 
-    image = (0, padded, 0, width)
-    stacks = [
-        to_owner(stack_images(rows[1], image), 0), to_owner(stack_images(last_rows, image), 1)
-    ]
-    acts = place_images(cfg, [rows[1], last_rows], stacks, (0, 0), LOW)
+    others = [swaps(rows[1]), swaps(last_rows)]
+    acts = place_images(cfg, [rows[1], last_rows], others, (0, 0), LOW)
     first_grads = relay_images(grad_rows[0])
-    stacks = [
-        to_owner(stack_images(first_grads, image), 0),
-        to_owner(stack_images(last_common, (0, padded, width, 2 * width)), 1),
-    ]
-    in_grads = place_images(cfg, [first_grads, last_common], stacks, (0, width), LOW).astype(F32)
+    others = [swaps(first_grads), swaps(last_common)]
+    in_grads = place_images(cfg, [first_grads, last_common], others, (0, width), LOW).astype(F32)
     ordered = order_attention_grads(cfg, pieces, piece.small)
     attention_final = place_attention_grads(cfg, ordered.own, swap(ordered.send))
     final_small = ordered.out
@@ -1335,8 +1311,8 @@
     return (
         acts,
         in_grads,
-        final_small[small][None],
-        final_small[small + 1][None],
+        final_small[experts + 2][None],
+        final_small[experts + 3][None],
         attention_final.qkv.transpose(0, 1, 3, 2),
         attention_final.out,
         final_small[experts][None],

time: 760 us -> 713 us (0.938)
  starting transfers between devices: 211 us -> 179 us
  Pallas kernels: 196 us -> 185 us
  waiting for transfers between devices: 296 us -> 285 us
    ppermute x45, waiting for transfers between devices: 198 us -> 151 us  [across(): return lax.ppermute(value, TENSOR, [(i, i ^ flip) for i in range(count)])]
    ppermute x13 -> x0, starting transfers between devices: 28.8 us -> none  [the longest x10 19.6 us: to_owner(): return lax.ppermute(value, SECTION, [(1 - layer, layer)])]
    ppermute x6, waiting for transfers between devices: 16.6 us -> 38.1 us  [along(): return lax.ppermute(value, EXPERT, [(i, i ^ flip) for i in range(count)])]
    pallas_call x32 -> x28, Pallas kernels: 196 us -> 185 us  [run(): pl.pallas_call(kernel, out_shape=tuple(shapes), in_specs=in_specs, out_sp...]
    ppermute x56, waiting for transfers between devices: 64.8 us -> 74.9 us  [hop(): return lax.ppermute(value, (EXPERT, TENSOR), pairs)]
    ppermute x66 -> x90, waiting for transfers between devices: 16.3 us -> 20.5 us  [swap(): return lax.ppermute(value, SECTION, [(0, 1), (1, 0)])]
    unnamed x361 -> x387, local copies, waits for them, and re-layouts: 19.1 us -> 22.3 us
    ppermute x66 -> x90, starting transfers between devices: 19.6 us -> 19.1 us  [swap(): return lax.ppermute(value, SECTION, [(0, 1), (1, 0)])]
  transfers between devices with their start and end apart: 186 -> 197, of which waited for: 55 -> 61; matrix products, arithmetic and copies ran while one was open for 5% -> 5% of each run, Pallas kernels for 23% -> 25%
where the time goes in v2:
time: 713 us; the launch traced here: 701 us
  waiting for transfers between devices  285 us (40%)
  Pallas kernels  185 us (26%)
  starting transfers between devices  179 us (25%)
  local copies, waits for them, and re-layouts  29.9 us (4%)
  other arithmetic  19.4 us (3%)
    pallas_call x28, Pallas kernels, run(): pl.pallas_call(kernel, out_shape=tuple(shapes), in_specs=in_specs, out_sp...  185 us
    ppermute x45, waiting for transfers between devices, across(): return lax.ppermute(value, TENSOR, [(i, i ^ flip) for i in range(count)])  151 us
    ppermute x56, starting transfers between devices, hop(): return lax.ppermute(value, (EXPERT, TENSOR), pairs)  97.4 us
    ppermute x56, waiting for transfers between devices, hop(): return lax.ppermute(value, (EXPERT, TENSOR), pairs)  74.9 us
    ppermute x45, starting transfers between devices, across(): return lax.ppermute(value, TENSOR, [(i, i ^ flip) for i in range(count)])  52 us
    ppermute x6, waiting for transfers between devices, along(): return lax.ppermute(value, EXPERT, [(i, i ^ flip) for i in range(count)])  38.1 us
    unnamed x387, local copies, waits for them, and re-layouts  22.3 us
    ppermute x90, waiting for transfers between devices, swap(): return lax.ppermute(value, SECTION, [(0, 1), (1, 0)])  20.5 us
  transfers between devices with their start and end apart: 197, of which 61 were waited for; matrix products, arithmetic and copies ran while one was open for 5% of the time, Pallas kernels for 25%

profile of v2, /device:TPU:0, one launch (start us, length us, event | category | flops | bytes accessed | tf_op | source)
XLA Modules:
  0.0 701.5 jit_solution(2515957492139884921)
XLA Ops:
  30.5 8.0 %shard_map.222 = (bf16[208,192]{1,0:T(8,128)(2,1)}, bf16[208,192]{1,0:T(8,128)(2,1)}, bf16[208,192]{1,0:T(8,128)(2,1)}, bf16[208,192]{1,0:T(8,128)(2,1)}, bf16[2...) custom-call(s32[4]{0:T(128)} %pad_add_fusion.refs_0_.refs_4_, ...), custom_call_target="tpu_custom_call" | custom-call | flops 1513095168 | bytes 5824560 | tf_op jit(solution)/shard_map/pallas_call | solution.py:102
  40.6 23.4 %collective-permute-done.4.refs_3_ = bf16[208,192]{1,0:T(8,128)(2,1)S(1)} collective-permute-done((bf16[208,192]{1,0:T(8,128)(2,1)}, bf16[208,192]{1,0:T(8,128)(2,1)S(1)}, u32[]{:S(2)}, u32[]{:S(2)}) %collective-permute-start.4) | collective-permute-done | bytes 79904 | tf_op jit(solution)/shard_map/ppermute | solution.py:30
  75.4 5.3 shard_map.223
  87.8 10.0 %collective-permute-done.47.refs_25_.refs_8_ = bf16[384,768]{1,0:T(8,128)(2,1)} collective-permute-done((bf16[384,768]{1,0:T(8,128)(2,1)}, bf16[384,768]{1,0:T(8,128)(2,1)}, u32[]{:S(2)}, u32[]{:S(2)}) %collective-permute-start.47) | collective-permute-done | bytes 589856 | tf_op jit(solution)/shard_map/ppermute | solution.py:30
  114.4 6.7 collective-permute-done.20.refs_6_
  135.5 12.0 %collective-permute-done.25.refs_12_.refs_15_ = bf16[768,768]{1,0:T(8,128)(2,1)} collective-permute-done((bf16[768,768]{1,0:T(8,128)(2,1)}, bf16[768,768]{1,0:T(8,128)(2,1)}, u32[]{:S(2)}, u32[]{:S(2)}) %collective-permute-start.25) | collective-permute-done | bytes 1179680 | tf_op jit(solution)/shard_map/ppermute | solution.py:30
  151.9 11.3 %shard_map.225 = (bf16[512,768]{1,0:T(8,128)(2,1)}, bf16[64,768]{1,0:T(8,128)(2,1)}, bf16[64,768]{1,0:T(8,128)(2,1)}, bf16[64,768]{1,0:T(8,128)(2,1)}, bf16[64,7...) custom-call(s32[4]{0:T(128)} %pad_add_fusion.refs_0_.refs_4_, ...), custom_call_target="tpu_custom_call" | custom-call | flops 4831838208 | bytes 18087952 | tf_op jit(solution)/shard_map/pallas_call | solution.py:102
  166.8 9.9 %collective-permute-done.65.refs_11_.refs_14_ = bf16[768,768]{1,0:T(8,128)(2,1)} collective-permute-done((bf16[768,768]{1,0:T(8,128)(2,1)}, bf16[768,768]{1,0:T(8,128)(2,1)}, u32[]{:S(2)}, u32[]{:S(2)}) %collective-permute-start.65) | collective-permute-done | bytes 1179680 | tf_op jit(solution)/shard_map/ppermute | solution.py:30
  179.3 22.2 %collective-permute-done.66.refs_12_.refs_15_ = bf16[768,768]{1,0:T(8,128)(2,1)} collective-permute-done((bf16[768,768]{1,0:T(8,128)(2,1)}, bf16[768,768]{1,0:T(8,128)(2,1)}, u32[]{:S(2)}, u32[]{:S(2)}) %collective-permute-start.66) | collective-permute-done | bytes 1179680 | tf_op jit(solution)/shard_map/ppermute | solution.py:30
  209.3 5.5 collective-permute-done.34.refs_8_
  228.0 10.9 %shard_map.226 = (bf16[208,768]{1,0:T(8,128)(2,1)}, bf16[2,208,768]{2,1,0:T(8,128)(2,1)}, f32[208,768]{1,0:T(8,128)}, bf16[208,768]{1,0:T(8,128)(2,1)}, f32[208,...) custom-call(s32[4]{0:T(128)} %pad_add_fusion.refs_0_.refs_4_, ...), custom_call_target="tpu_custom_call" | custom-call | flops 1513095168 | bytes 10494992 | tf_op jit(solution)/shard_map/pallas_call | solution.py:102
  266.3 8.8 %collective-permute-done.59.refs_5_ = bf16[64,768]{1,0:T(8,128)(2,1)S(1)} collective-permute-done((bf16[64,768]{1,0:T(8,128)(2,1)}, bf16[64,768]{1,0:T(8,128)(2,1)S(1)}, u32[]{:S(2)}, u32[]{:S(2)}) %collective-permute-start.59) | collective-permute-done | bytes 98336 | tf_op jit(solution)/shard_map/ppermute | solution.py:45
  284.6 11.5 %shard_map.228 = (bf16[512,768]{1,0:T(8,128)(2,1)}, bf16[64,768]{1,0:T(8,128)(2,1)}, bf16[64,768]{1,0:T(8,128)(2,1)}, bf16[64,768]{1,0:T(8,128)(2,1)}, bf16[64,7...) custom-call(s32[4]{0:T(128)} %pad_add_fusion.refs_0_.refs_4_, ...), custom_call_target="tpu_custom_call" | custom-call | flops 4831838208 | bytes 18087952 | tf_op jit(solution)/shard_map/pallas_call | solution.py:102
  300.4 13.4 %shard_map.232 = (bf16[512,768]{1,0:T(8,128)(2,1)}, bf16[64,768]{1,0:T(8,128)(2,1)}, bf16[64,768]{1,0:T(8,128)(2,1)}, bf16[64,768]{1,0:T(8,128)(2,1)}, bf16[64,7...) custom-call(s32[4]{0:T(128)} %pad_add_fusion.refs_0_.refs_4_, ...), custom_call_target="tpu_custom_call" | custom-call | flops 4831838208 | bytes 25952272 | tf_op jit(solution)/shard_map/pallas_call | solution.py:102
  371.8 12.0 %shard_map.234 = (bf16[208,768]{1,0:T(8,128)(2,1)}, bf16[240,1536]{1,0:T(8,128)(2,1)}, bf16[208,768]{1,0:T(8,128)(2,1)}, bf16[208,768]{1,0:T(8,128)(2,1)}, bf16[...) custom-call(s32[4]{0:T(128)} %pad_add_fusion.refs_0_.refs_4_, bf16[208,768]{1,0:T(8,128)(2,1)} %get-tuple-element.189.refs_2_.refs_1_, ...), custom_call_target="tpu_custom_call" | custom-call | flops 3026190336 | bytes 9777168 | tf_op jit(solution)/shard_map/pallas_call | solution.py:102
  415.4 5.4 collective-permute-done.126.refs_6_
  423.2 13.3 %shard_map.236 = (bf16[512,768]{1,0:T(8,128)(2,1)}, bf16[64,768]{1,0:T(8,128)(2,1)}, bf16[64,768]{1,0:T(8,128)(2,1)}, bf16[64,768]{1,0:T(8,128)(2,1)}, bf16[64,7...) custom-call(s32[4]{0:T(128)} %pad_add_fusion.refs_0_.refs_4_, ...), custom_call_target="tpu_custom_call" | custom-call | flops 4831838208 | bytes 25952272 | tf_op jit(solution)/shard_map/pallas_call | solution.py:102
  470.1 8.2 %collective-permute-done.88.refs_9_ = bf16[208,768]{1,0:T(8,128)(2,1)S(1)} collective-permute-done((bf16[208,768]{1,0:T(8,128)(2,1)S(1)}, bf16[208,768]{1,0:T(8,128)(2,1)S(1)}, u32[]{:S(2)}, u32[]{:S(2)}) %collective-permute-start.88) | collective-permute-done | bytes 319520 | tf_op jit(solution)/shard_map/ppermute | solution.py:30
  486.1 13.3 %shard_map.238 = (bf16[208,768]{1,0:T(8,128)(2,1)}, bf16[240,576]{1,0:T(8,128)(2,1)}, bf16[240,576]{1,0:T(8,128)(2,1)}, bf16[240,576]{1,0:T(8,128)(2,1)}, bf16[240,576]{1,0:T(8,128)(2,1)}) custom-call(s32[4]{0:T(128)} %pad_add_fusion.refs_0_.refs_4_, bf16[208,768]{1,0:T(8,128)(2,1)} %get-tuple-element.163.refs_1_, ...), custom_call_target="tpu_custom_call" | custom-call | flops 3026190336 | bytes 7483408 | tf_op jit(solution)/shard_map/pallas_call | solution.py:102
  503.0 6.9 collective-permute-done.165.refs_6_
  510.7 5.7 collective-permute-done.166.refs_7_
  525.5 7.8 %collective-permute-done.168.refs_10_ = bf16[224,768]{1,0:T(8,128)(2,1)S(1)} collective-permute-done((bf16[224,768]{1,0:T(8,128)(2,1)S(1)}, bf16[224,768]{1,0:T(8,128)(2,1)S(1)}, u32[]{:S(2)}, u32[]{:S(2)}) %collective-permute-start.168) | collective-permute-done | bytes 344096 | tf_op jit(solution)/shard_map/ppermute | solution.py:30
  536.0 10.6 %shard_map.247 = (bf16[768,768]{1,0:T(8,128)(2,1)}, bf16[768,768]{1,0:T(8,128)(2,1)}, bf16[768,768]{1,0:T(8,128)(2,1)}, bf16[768,768]{1,0:T(8,128)(2,1)}) custom-call(s32[4]{0:T(128)} %pad_add_fusion.refs_0_.refs_4_, bf16[512,768]{1,0:T(8,128)(2,1)} %get-tuple-element.221.refs_9_.refs_1_, bf16[512,768]{1,0:T(8,128)(2,1)} %get-tuple-element.301.refs_2_, ...), custom_call_target="tpu_custom_call" | custom-call | flops 4831838208 | bytes 16515088 | tf_op jit(solution)/shard_map/pallas_call | solution.py:102
  549.1 10.6 %shard_map.246 = (bf16[768,768]{1,0:T(8,128)(2,1)}, bf16[768,768]{1,0:T(8,128)(2,1)}, bf16[768,768]{1,0:T(8,128)(2,1)}, bf16[768,768]{1,0:T(8,128)(2,1)}) custom-call(s32[4]{0:T(128)} %pad_add_fusion.refs_0_.refs_4_, bf16[512,768]{1,0:T(8,128)(2,1)} %get-tuple-element.251.refs_9_.refs_1_, bf16[512,768]{1,0:T(8,128)(2,1)} %get-tuple-element.293.refs_2_, ...), custom_call_target="tpu_custom_call" | custom-call | flops 4831838208 | bytes 16515088 | tf_op jit(solution)/shard_map/pallas_call | solution.py:102
  559.7 6.1 collective-permute-done.153.refs_5_
  566.8 5.6 shard_map.240
  573.2 6.1 shard_map.241
  590.4 12.1 %collective-permute-done.186 = bf16[768,768]{1,0:T(8,128)(2,1)} collective-permute-done((bf16[768,768]{1,0:T(8,128)(2,1)}, bf16[768,768]{1,0:T(8,128)(2,1)}, u32[]{:S(2)}, u32[]{:S(2)}) %collective-permute-start.186) | collective-permute-done | bytes 1179680 | tf_op jit(solution)/shard_map/ppermute | solution.py:30
  607.3 10.9 %collective-permute-done.177.refs_2_ = bf16[2,112,768]{2,1,0:T(8,128)(2,1)S(1)} collective-permute-done((bf16[2,112,768]{2,1,0:T(8,128)(2,1)S(1)}, bf16[2,112,768]{2,1,0:T(8,128)(2,1)S(1)}, u32[]{:S(2)}, u32[]{:S(2)}) %collective-permute-start.177) | collective-permute-done | bytes 344096 | tf_op jit(solution)/shard_map/ppermute | solution.py:35
  620.3 9.8 %collective-permute-done.178.refs_3_ = bf16[2,112,768]{2,1,0:T(8,128)(2,1)S(1)} collective-permute-done((bf16[2,112,768]{2,1,0:T(8,128)(2,1)S(1)}, bf16[2,112,768]{2,1,0:T(8,128)(2,1)S(1)}, u32[]{:S(2)}, u32[]{:S(2)}) %collective-permute-start.178) | collective-permute-done | bytes 344096 | tf_op jit(solution)/shard_map/ppermute | solution.py:35
  655.6 12.0 %collective-permute-done.180.refs_3_ = bf16[2,96,768]{2,1,0:T(8,128)(2,1)S(1)} collective-permute-done((bf16[2,96,768]{2,1,0:T(8,128)(2,1)S(1)}, bf16[2,96,768]{2,1,0:T(8,128)(2,1)S(1)}, u32[]{:S(2)}, u32[]{:S(2)}) %collective-permute-start.180) | collective-permute-done | bytes 294944 | tf_op jit(solution)/shard_map/ppermute | solution.py:35
  694.3 6.8 shard_map.248
  (797 shorter events, 376.4 us)
Async XLA Ops:
  4.5 93.3 %collective-permute-start.63 = (bf16[2,768,768]{2,1,0:T(8,128)(2,1)}, bf16[2,768,768]{2,1,0:T(8,128)(2,1)}, u32[]{:S(2)}, u32[]{:S(2)}) collective-permute-start(bf16[2,768,768]{2,1,0:T(8,128)(2,1)} %bitcast.45), channel_id=1, source_target_pairs={{0,16},{16,0},{1,17},{17,1},{2,18},{18,2},{3,19},{19,3},{4,20},{20... | collective-permute-start | bytes 7077896 | tf_op jit(solution)/shard_map/ppermute | solution.py:25
  19.3 64.8 %collective-permute-start.23 = (bf16[768,768]{1,0:T(8,128)(2,1)}, bf16[768,768]{1,0:T(8,128)(2,1)}, u32[]{:S(2)}, u32[]{:S(2)}) collective-permute-start(bf16[768,768]{1,0:T(8,128)(2,1)} %get-tuple-element.324), channel_id=1, source_target_pairs={{0,1},{1,0},{2,3},{3,2},{4,5},{5,4},{6,7},{7,6},{8,9},{9,8},{10,11... | collective-permute-start | bytes 3538952 | tf_op jit(solution)/shard_map/ppermute | solution.py:30
  26.5 54.3 %collective-permute-start.45 = (bf16[384,768]{1,0:T(8,128)(2,1)S(1)}, bf16[384,768]{1,0:T(8,128)(2,1)}, u32[]{:S(2)}, u32[]{:S(2)}) collective-permute-start(bf16[384,768]{1,0:T(8,128)(2,1)S(1)} %maximum_select_fusion.refs_22_.refs_5_), channel_id=1, source_target_pairs={{0,1},{1,0},{2,3},{3,2},{4,5},{5,4},{6,7},{7,6},{8,9},{9,8},{10,11... | collective-permute-start | bytes 1769480 | tf_op jit(solution)/shard_map/ppermute | solution.py:30
  30.0 51.3 %collective-permute-start.46 = (bf16[384,768]{1,0:T(8,128)(2,1)S(1)}, bf16[384,768]{1,0:T(8,128)(2,1)}, u32[]{:S(2)}, u32[]{:S(2)}) collective-permute-start(bf16[384,768]{1,0:T(8,128)(2,1)S(1)} %maximum_select_fusion.refs_22_.refs_5_), channel_id=1, source_target_pairs={{0,2},{1,3},{2,0},{3,1},{4,6},{5,7},{6,4},{7,5},{8,10},{9,11},{10,... | collective-permute-start | bytes 1769480 | tf_op jit(solution)/shard_map/ppermute | solution.py:30
  82.8 52.2 %collective-permute-start.24 = (bf16[768,768]{1,0:T(8,128)(2,1)}, bf16[768,768]{1,0:T(8,128)(2,1)}, u32[]{:S(2)}, u32[]{:S(2)}) collective-permute-start(bf16[768,768]{1,0:T(8,128)(2,1)} %get-tuple-element.325.refs_9_.refs_12_), channel_id=1, source_target_pairs={{0,2},{1,3},{2,0},{3,1},{4,6},{5,7},{6,4},{7,5},{8,10},{9,11},{10,... | collective-permute-start | bytes 3538952 | tf_op jit(solution)/shard_map/ppermute | solution.py:30
  84.1 63.4 %collective-permute-start.25 = (bf16[768,768]{1,0:T(8,128)(2,1)}, bf16[768,768]{1,0:T(8,128)(2,1)}, u32[]{:S(2)}, u32[]{:S(2)}) collective-permute-start(bf16[768,768]{1,0:T(8,128)(2,1)} %collective-permute-done.23.refs_10_.refs_13_), channel_id=1, source_target_pairs={{0,2},{1,3},{2,0},{3,1},{4,6},{5,7},{6,4},{7,5},{8,10},{9,11},{10,... | collective-permute-start | bytes 3538952 | tf_op jit(solution)/shard_map/ppermute | solution.py:30
  97.8 49.7 %collective-permute-start.26 = (bf16[768,768]{1,0:T(8,128)(2,1)}, bf16[768,768]{1,0:T(8,128)(2,1)S(1)}, u32[]{:S(2)}, u32[]{:S(2)}) collective-permute-start(bf16[768,768]{1,0:T(8,128)(2,1)} %get-tuple-element.325.refs_9_.refs_12_), channel_id=1, source_target_pairs={{0,16},{16,0},{1,17},{17,1},{2,18},{18,2},{3,19},{19,3},{4,20},{20... | collective-permute-start | bytes 3538952 | tf_op jit(solution)/shard_map/ppermute | solution.py:25
  103.7 45.4 %collective-permute-start.64 = (bf16[768,768]{1,0:T(8,128)(2,1)S(1)}, bf16[768,768]{1,0:T(8,128)(2,1)}, u32[]{:S(2)}, u32[]{:S(2)}) collective-permute-start(bf16[768,768]{1,0:T(8,128)(2,1)S(1)} %get-tuple-element.322), channel_id=1, source_target_pairs={{0,1},{1,0},{2,3},{3,2},{4,5},{5,4},{6,7},{7,6},{8,9},{9,8},{10,11... | collective-permute-start | bytes 3538952 | tf_op jit(solution)/shard_map/ppermute | solution.py:30
  147.5 29.2 %collective-permute-start.65 = (bf16[768,768]{1,0:T(8,128)(2,1)}, bf16[768,768]{1,0:T(8,128)(2,1)}, u32[]{:S(2)}, u32[]{:S(2)}) collective-permute-start(bf16[768,768]{1,0:T(8,128)(2,1)} %get-tuple-element.323.refs_9_.refs_12_), channel_id=1, source_target_pairs={{0,2},{1,3},{2,0},{3,1},{4,6},{5,7},{6,4},{7,5},{8,10},{9,11},{10,... | collective-permute-start | bytes 3538952 | tf_op jit(solution)/shard_map/ppermute | solution.py:30
  149.1 52.4 %collective-permute-start.66 = (bf16[768,768]{1,0:T(8,128)(2,1)}, bf16[768,768]{1,0:T(8,128)(2,1)}, u32[]{:S(2)}, u32[]{:S(2)}) collective-permute-start(bf16[768,768]{1,0:T(8,128)(2,1)} %collective-permute-done.64.refs_10_.refs_13_), channel_id=1, source_target_pairs={{0,2},{1,3},{2,0},{3,1},{4,6},{5,7},{6,4},{7,5},{8,10},{9,11},{10,... | collective-permute-start | bytes 3538952 | tf_op jit(solution)/shard_map/ppermute | solution.py:30
  163.2 40.8 %collective-permute-start.30 = (bf16[64,768]{1,0:T(8,128)(2,1)}, bf16[64,768]{1,0:T(8,128)(2,1)S(1)}, u32[]{:S(2)}, u32[]{:S(2)}) collective-permute-start(bf16[64,768]{1,0:T(8,128)(2,1)} %get-tuple-element.180), channel_id=1, source_target_pairs={{0,1},{1,0},{2,3},{3,2},{4,5},{5,4},{6,7},{7,6},{8,9},{9,8},{10,11... | collective-permute-start | bytes 294920 | tf_op jit(solution)/shard_map/ppermute | solution.py:45
  163.7 41.7 %collective-permute-start.31 = (bf16[64,768]{1,0:T(8,128)(2,1)}, bf16[64,768]{1,0:T(8,128)(2,1)S(1)}, u32[]{:S(2)}, u32[]{:S(2)}) collective-permute-start(bf16[64,768]{1,0:T(8,128)(2,1)} %get-tuple-element.181), channel_id=1, source_target_pairs={{0,4},{1,5},{2,6},{3,7},{4,0},{5,1},{6,2},{7,3},{8,12},{9,13},{10,... | collective-permute-start | bytes 294920 | tf_op jit(solution)/shard_map/ppermute | solution.py:45
  165.4 43.4 %collective-permute-start.32 = (bf16[64,768]{1,0:T(8,128)(2,1)}, bf16[64,768]{1,0:T(8,128)(2,1)S(1)}, u32[]{:S(2)}, u32[]{:S(2)}) collective-permute-start(bf16[64,768]{1,0:T(8,128)(2,1)} %get-tuple-element.182), channel_id=1, source_target_pairs={{0,5},{1,4},{2,7},{3,6},{4,1},{5,0},{6,3},{7,2},{8,13},{9,12},{10,... | collective-permute-start | bytes 294920 | tf_op jit(solution)/shard_map/ppermute | solution.py:45
  176.7 32.1 %collective-permute-start.33 = (bf16[64,768]{1,0:T(8,128)(2,1)}, bf16[64,768]{1,0:T(8,128)(2,1)S(1)}, u32[]{:S(2)}, u32[]{:S(2)}) collective-permute-start(bf16[64,768]{1,0:T(8,128)(2,1)} %get-tuple-element.183), channel_id=1, source_target_pairs={{0,8},{1,9},{2,10},{3,11},{4,12},{5,13},{6,14},{7,15},{8,0},{9,1},... | collective-permute-start | bytes 294920 | tf_op jit(solution)/shard_map/ppermute | solution.py:45
  214.9 36.7 %collective-permute-start.67 = (bf16[768,768]{1,0:T(8,128)(2,1)}, bf16[768,768]{1,0:T(8,128)(2,1)}, u32[]{:S(2)}, u32[]{:S(2)}) collective-permute-start(bf16[768,768]{1,0:T(8,128)(2,1)} %get-tuple-element.323.refs_9_.refs_12_), channel_id=1, source_target_pairs={{0,16},{16,0},{1,17},{17,1},{2,18},{18,2},{3,19},{19,3},{4,20},{20... | collective-permute-start | bytes 3538952 | tf_op jit(solution)/shard_map/ppermute | solution.py:25
  215.4 38.6 %collective-permute-start.68 = (bf16[768,768]{1,0:T(8,128)(2,1)}, bf16[768,768]{1,0:T(8,128)(2,1)}, u32[]{:S(2)}, u32[]{:S(2)}) collective-permute-start(bf16[768,768]{1,0:T(8,128)(2,1)} %collective-permute-done.64.refs_10_.refs_13_), channel_id=1, source_target_pairs={{0,16},{16,0},{1,17},{17,1},{2,18},{18,2},{3,19},{19,3},{4,20},{20... | collective-permute-start | bytes 3538952 | tf_op jit(solution)/shard_map/ppermute | solution.py:25
  215.5 39.0 %collective-permute-start.69 = (bf16[768,768]{1,0:T(8,128)(2,1)}, bf16[768,768]{1,0:T(8,128)(2,1)}, u32[]{:S(2)}, u32[]{:S(2)}) collective-permute-start(bf16[768,768]{1,0:T(8,128)(2,1)} %collective-permute-done.65.refs_11_.refs_14_), channel_id=1, source_target_pairs={{0,16},{16,0},{1,17},{17,1},{2,18},{18,2},{3,19},{19,3},{4,20},{20... | collective-permute-start | bytes 3538952 | tf_op jit(solution)/shard_map/ppermute | solution.py:25
  216.2 40.7 %collective-permute-start.70 = (bf16[768,768]{1,0:T(8,128)(2,1)}, bf16[768,768]{1,0:T(8,128)(2,1)}, u32[]{:S(2)}, u32[]{:S(2)}) collective-permute-start(bf16[768,768]{1,0:T(8,128)(2,1)} %collective-permute-done.66.refs_12_.refs_15_), channel_id=1, source_target_pairs={{0,16},{16,0},{1,17},{17,1},{2,18},{18,2},{3,19},{19,3},{4,20},{20... | collective-permute-start | bytes 3538952 | tf_op jit(solution)/shard_map/ppermute | solution.py:25
  266.2 29.9 %collective-permute-start.102 = (bf16[64,768]{1,0:T(8,128)(2,1)S(1)}, bf16[64,768]{1,0:T(8,128)(2,1)S(1)}, u32[]{:S(2)}, u32[]{:S(2)}) collective-permute-start(bf16[64,768]{1,0:T(8,128)(2,1)S(1)} %copy-done.160), channel_id=1, source_target_pairs={{0,9},{1,8},{2,11},{3,10},{4,13},{5,12},{6,15},{7,14},{8,1},{9,0},... | collective-permute-start | bytes 294920 | tf_op jit(solution)/shard_map/ppermute | solution.py:45
  414.9 119.9 %collective-permute-start.189 = (bf16[4,512,768]{2,1,0:T(8,128)(2,1)}, bf16[4,512,768]{2,1,0:T(8,128)(2,1)}, u32[]{:S(2)}, u32[]{:S(2)}) collective-permute-start(bf16[4,512,768]{2,1,0:T(8,128)(2,1)} %get-tuple-element.304), channel_id=1, source_target_pairs={{0,16},{16,0},{1,17},{17,1},{2,18},{18,2},{3,19},{19,3},{4,20},{20... | collective-permute-start | bytes 9437192 | tf_op jit(solution)/shard_map/ppermute | solution.py:25
  414.9 51.3 %collective-permute-start.188 = (bf16[512,768]{1,0:T(8,128)(2,1)}, bf16[512,768]{1,0:T(8,128)(2,1)}, u32[]{:S(2)}, u32[]{:S(2)}) collective-permute-start(bf16[512,768]{1,0:T(8,128)(2,1)} %get-tuple-element.303), channel_id=1, source_target_pairs={{0,16},{16,0},{1,17},{17,1},{2,18},{18,2},{3,19},{19,3},{4,20},{20... | collective-permute-start | bytes 2359304 | tf_op jit(solution)/shard_map/ppermute | solution.py:25
  436.6 111.5 %collective-permute-start.184 = (bf16[4,512,768]{2,1,0:T(8,128)(2,1)}, bf16[4,512,768]{2,1,0:T(8,128)(2,1)}, u32[]{:S(2)}, u32[]{:S(2)}) collective-permute-start(bf16[4,512,768]{2,1,0:T(8,128)(2,1)} %get-tuple-element.296), channel_id=1, source_target_pairs={{0,16},{16,0},{1,17},{17,1},{2,18},{18,2},{3,19},{19,3},{4,20},{20... | collective-permute-start | bytes 9437192 | tf_op jit(solution)/shard_map/ppermute | solution.py:25
  534.8 37.6 %collective-permute-start.156 = (bf16[240,1536]{1,0:T(8,128)(2,1)S(1)}, bf16[240,1536]{1,0:T(8,128)(2,1)S(1)}, u32[]{:S(2)}, u32[]{:S(2)}) collective-permute-start(bf16[240,1536]{1,0:T(8,128)(2,1)S(1)} %collective-permute-done.155.refs_8_.refs_11_), channel_id=1, source_target_pairs={{0,1},{1,0},{2,3},{3,2},{4,5},{5,4},{6,7},{7,6},{8,9},{9,8},{10,11... | collective-permute-start | bytes 2211848 | tf_op jit(solution)/shard_map/ppermute | solution.py:30
  547.6 31.8 %collective-permute-start.159 = (bf16[208,768]{1,0:T(8,128)(2,1)}, bf16[208,768]{1,0:T(8,128)(2,1)S(1)}, u32[]{:S(2)}, u32[]{:S(2)}) collective-permute-start(bf16[208,768]{1,0:T(8,128)(2,1)} %collective-permute-done.152.refs_4_), channel_id=1, source_target_pairs={{0,16},{16,0},{1,17},{17,1},{2,18},{18,2},{3,19},{19,3},{4,20},{20... | collective-permute-start | bytes 958472 | tf_op jit(solution)/shard_map/ppermute | solution.py:25
  548.1 38.4 %collective-permute-start.191 = (bf16[768,768]{1,0:T(8,128)(2,1)}, bf16[768,768]{1,0:T(8,128)(2,1)}, u32[]{:S(2)}, u32[]{:S(2)}) collective-permute-start(bf16[768,768]{1,0:T(8,128)(2,1)} %get-tuple-element.308), channel_id=1, source_target_pairs={{0,2},{1,3},{2,0},{3,1},{4,6},{5,7},{6,4},{7,5},{8,10},{9,11},{10,... | collective-permute-start | bytes 3538952 | tf_op jit(solution)/shard_map/ppermute | solution.py:30
  565.8 36.7 %collective-permute-start.186 = (bf16[768,768]{1,0:T(8,128)(2,1)}, bf16[768,768]{1,0:T(8,128)(2,1)}, u32[]{:S(2)}, u32[]{:S(2)}) collective-permute-start(bf16[768,768]{1,0:T(8,128)(2,1)} %get-tuple-element.300), channel_id=1, source_target_pairs={{0,2},{1,3},{2,0},{3,1},{4,6},{5,7},{6,4},{7,5},{8,10},{9,11},{10,... | collective-permute-start | bytes 3538952 | tf_op jit(solution)/shard_map/ppermute | solution.py:30
  581.7 51.3 %collective-permute-start.190 = (bf16[768,768]{1,0:T(8,128)(2,1)}, bf16[768,768]{1,0:T(8,128)(2,1)}, u32[]{:S(2)}, u32[]{:S(2)}) collective-permute-start(bf16[768,768]{1,0:T(8,128)(2,1)} %get-tuple-element.306), channel_id=1, source_target_pairs={{0,2},{1,3},{2,0},{3,1},{4,6},{5,7},{6,4},{7,5},{8,10},{9,11},{10,... | collective-permute-start | bytes 3538952 | tf_op jit(solution)/shard_map/ppermute | solution.py:30
  586.4 65.7 %collective-permute-start.185 = (bf16[768,768]{1,0:T(8,128)(2,1)}, bf16[768,768]{1,0:T(8,128)(2,1)}, u32[]{:S(2)}, u32[]{:S(2)}) collective-permute-start(bf16[768,768]{1,0:T(8,128)(2,1)} %get-tuple-element.298), channel_id=1, source_target_pairs={{0,2},{1,3},{2,0},{3,1},{4,6},{5,7},{6,4},{7,5},{8,10},{9,11},{10,... | collective-permute-start | bytes 3538952 | tf_op jit(solution)/shard_map/ppermute | solution.py:30
  605.2 63.9 %collective-permute-start.192 = (bf16[768,768]{1,0:T(8,128)(2,1)}, bf16[768,768]{1,0:T(8,128)(2,1)}, u32[]{:S(2)}, u32[]{:S(2)}) collective-permute-start(bf16[768,768]{1,0:T(8,128)(2,1)} %add_convert_fusion), channel_id=1, source_target_pairs={{0,1},{1,0},{2,3},{3,2},{4,5},{5,4},{6,7},{7,6},{8,9},{9,8},{10,11... | collective-permute-start | bytes 3538952 | tf_op jit(solution)/shard_map/ppermute | solution.py:30
  606.5 62.6 %collective-permute-start.187 = (bf16[768,768]{1,0:T(8,128)(2,1)}, bf16[768,768]{1,0:T(8,128)(2,1)}, u32[]{:S(2)}, u32[]{:S(2)}) collective-permute-start(bf16[768,768]{1,0:T(8,128)(2,1)} %add_convert_fusion.2), channel_id=1, source_target_pairs={{0,1},{1,0},{2,3},{3,2},{4,5},{5,4},{6,7},{7,6},{8,9},{9,8},{10,11... | collective-permute-start | bytes 3538952 | tf_op jit(solution)/shard_map/ppermute | solution.py:30
  639.5 32.6 %collective-permute-start.164 = (bf16[240,1536]{1,0:T(8,128)(2,1)S(1)}, bf16[240,1536]{1,0:T(8,128)(2,1)}, u32[]{:S(2)}, u32[]{:S(2)}) collective-permute-start(bf16[240,1536]{1,0:T(8,128)(2,1)S(1)} %copy-done.7), channel_id=1, source_target_pairs={{0,16},{16,0},{1,17},{17,1},{2,18},{18,2},{3,19},{19,3},{4,20},{20... | collective-permute-start | bytes 2211848 | tf_op jit(solution)/shard_map/ppermute | solution.py:25
  667.6 26.6 %collective-permute-start.195 = (bf16[768,768]{1,0:T(8,128)(2,1)S(1)}, bf16[768,768]{1,0:T(8,128)(2,1)}, u32[]{:S(2)}, u32[]{:S(2)}) collective-permute-start(bf16[768,768]{1,0:T(8,128)(2,1)S(1)} %add_convert_fusion.1.refs_3_), channel_id=1, source_target_pairs={{0,16},{16,0},{1,17},{17,1},{2,18},{18,2},{3,19},{19,3},{4,20},{20... | collective-permute-start | bytes 3538952 | tf_op jit(solution)/shard_map/ppermute | solution.py:25
  (357 other events, 4972.5 us)
